TPU v7x, 256 devices: a whole 4x4x8 slice. The times are simulated.
256 devices in a mesh: grp: 4 (over y), dom: 64 (over x, z, core).
Axes of the slice: x: 4, y: 4, z: 8, core: 2. Of those that a mesh axis runs over, the one named last changes fastest.
Arguments:
- features: bfloat16 [786432, 256], P(('grp', 'dom')), may hold values from -6 to 6
- boundary_cache: float32 [65536, 256], P(('grp', 'dom')), may hold values from -6 to 6
- adjacency: bfloat16 [6144, 2, 128, 128], P(('grp', 'dom')), may hold values from -0.375 to 0.375
- neighbor: int32 [6144, 2], P(('grp', 'dom')), may hold values from 0 to 87
- counts: int32 [6144], P(('grp', 'dom')), may hold values from 1 to 2
- wanted: int32 [256, 64], P(('grp', 'dom')), may hold values from 0 to 1
- weight_in: bfloat16 [512, 512], replicated, may hold values from -0.25 to 0.25
- weight_out: bfloat16 [512, 256], replicated, may hold values from -0.25 to 0.25
- cotangent: bfloat16 [786432, 256], P(('grp', 'dom')), may hold values from -6 to 6
Outputs:
- grad_features: bfloat16 [786432, 256], P(('grp', 'dom'))
- grad_weight_in: float32 [512, 512], P('dom')
- grad_weight_out: float32 [512, 256], P('dom')
Inputs may be any that keep to these rules, and one draw needn't show every extreme that they name: `neighbor`: A value under 24 names a block of the same partition; a value 24 + q names the boundary block that the partition reads from partition q of its group. Slots from counts[b] on are padding and carry no edges.
All inputs are finite; a program needn't handle non-finite values.
Results may differ from a plain program's by a relative error of at most 0.0054.
Values may be sent and summed in bfloat16 or wider, within the bound.
No kernel may reach another device: no remote copies, remote signals or barrier semaphores. Data moves between devices by JAX's collectives and lax.ppermute only.
A program may use at most 128 MiB of HBM per device.

v0:
```python
import math

import jax
import jax.numpy as jnp
from jax import lax
from jax.experimental import pallas as pl
from jax.experimental.pallas import tpu as pltpu
from jax.sharding import PartitionSpec as P


NX, NZ, NC = 4, 8, 2


def place(x, z, c):
    return (x % NX) * (NZ * NC) + (z % NZ) * NC + c


def move(a, dx=0, dz=0, dc=0):
    pairs = [
        (place(x, z, c), place(x + dx, z + dz, c ^ dc))
        for x in range(NX)
        for z in range(NZ)
        for c in range(NC)
    ]
    return lax.ppermute(a, "dom", pairs)


BF = jnp.bfloat16
F32 = jnp.float32
WIRE = jnp.bfloat16
PER = 6


class Table:
    def __init__(self):
        self.arrays, self.spots = [], {}

    def add(self, array, xs, dz):
        self.arrays.append(array)
        for i, dx in enumerate(xs):
            self.spots[dx % NX, dz % NZ] = (len(self.arrays) - 1, 2 * i)


def gather_plane(own):
    near = Table()

    def go(a, **step):
        return move(a, **step)

    c1, c2, c3 = go(own, dx=1), go(own, dx=-1), go(own, dx=2)
    p, q = jnp.concatenate([own, c2]), jnp.concatenate([c1, c3])
    px, qx = (0, 1), (-1, 2)
    near.add(p, px, 0)
    near.add(q, qx, 0)
    pp, pm, qp, qm = p, p, q, q
    for k in (1, 2, 3):
        pp, pm = go(pp, dz=1), go(pm, dz=-1)
        qp, qm = go(qp, dz=1), go(qm, dz=-1)
        near.add(pp, px, -k)
        near.add(pm, px, k)
        near.add(qp, qx, -k)
        near.add(qm, qx, k)
    p4 = go(pp, dz=1)
    given_p = move(p4, dc=1)
    q4 = go(qm, dz=-1)
    given_q = move(q4, dc=1)
    return near, (p4, q4, given_p, given_q)


def pick(table, wants, position):
    block = table.arrays[0].shape[1:]
    spots = sorted(table.spots)
    count, sides = len(spots), len(wants)

    def kernel(*refs):
        want_refs, at_ref, pieces = refs[:sides], refs[sides], refs[sides + 1 : -sides - 2]
        outs, buf, sems = refs[-sides - 2 : -2], refs[-2], refs[-1]
        mx, mz, mc = at_ref[0], at_ref[1], at_ref[2]

        def take(o, i, e):
            n, k = table.spots[spots[i]]
            return pltpu.make_async_copy(pieces[n].at[k + e], buf.at[o, i], sems.at[0, o, i])

        def put(o, i):
            return pltpu.make_async_copy(buf.at[o, i], outs[o].at[i], sems.at[1, o, i])

        every = [(o, i) for o in range(sides) for i in range(count)]
        for o, i in every:
            dx, dz = spots[i]
            take(o, i, want_refs[o][0, place_of(mx + dx, mz + dz, mc)]).start()

        for o, i in every:
            take(o, i, 0).wait()
            put(o, i).start()
        for o, i in every:
            put(o, i).wait()

    return pl.pallas_call(
        kernel,
        out_shape=[jax.ShapeDtypeStruct((count, *block), BF)] * sides,
        in_specs=[pl.BlockSpec(memory_space=pltpu.SMEM)] * (sides + 1)
        + [pl.BlockSpec(memory_space=pl.ANY)] * len(table.arrays),
        out_specs=[pl.BlockSpec(memory_space=pl.ANY)] * sides,
        scratch_shapes=[pltpu.VMEM((sides, count, *block), BF), pltpu.SemaphoreType.DMA((2, sides, count))],
        name="pick",
    )(*wants, position, *table.arrays)


def place_of(x, z, c):
    x = jnp.where(x >= NX, x - NX, x)
    z = jnp.where(z >= NZ, z - NZ, z)
    return x * (NZ * NC) + z * NC + c


def dot(a, b, ca, cb):
    return lax.dot_general(a, b, (((ca,), (cb,)), ((), ())), preferred_element_type=F32)


def forward(features, blocks, adjacency, cotangent, weight_in, weight_out, neighbor, counts, wanted, position, scale):
    nblocks, slots, rows, _ = adjacency.shape
    nodes, channels = features.shape
    hid = weight_in.shape[1]
    per = PER
    tile = per * rows
    steps = nblocks // per

    def kernel(
        nb_ref, cnt_ref, want_ref, at_ref, owned, kept, given, p4, q4, given_p, given_q, adj, feat, cot, win, wout,
        gp_out, keep, send, src, joined, acc_in, acc_out, sems,
    ):
        step = pl.program_id(0)
        mx, mz, mc = at_ref[0], at_ref[1], at_ref[2]

        def slot(b, s):
            return src.at[b, pl.ds(s * rows, rows)]

        def fetch(b, s):
            nb = nb_ref[b, s]
            live = s < cnt_ref[b]
            local = nb < nblocks
            q = jnp.maximum(nb - nblocks, 0)
            qx, qz, qc = q >> 4, (q >> 1) & 7, q & 1
            dx, dz = (qx - mx) & 3, (qz - mz) & 7
            far = dz == 4
            rel = dx * 7 + jnp.where(dz > 4, dz - 1, jnp.minimum(dz, 3))
            e = want_ref[0, q]

            def start(ref):
                pltpu.make_async_copy(ref, slot(b, s), sems.at[b, s]).start()

            def start_from(table, tp, tq):
                @pl.when(jnp.logical_not(far))
                def _():
                    start(table.at[rel])

                @pl.when(far)
                def _():
                    @pl.when(dx < 2)
                    def _():
                        start(tp.at[2 * dx + e])

                    @pl.when(dx >= 2)
                    def _():
                        start(tq.at[2 * (3 - dx) + e])

            @pl.when(live)
            def _():
                @pl.when(local)
                def _():
                    start(owned.at[pl.ds(pl.multiple_of(jnp.minimum(nb, nblocks - 1) * rows, rows), rows)])

                @pl.when(jnp.logical_not(local))
                def _():
                    @pl.when(qc == mc)
                    def _():
                        start_from(kept, p4, q4)

                    @pl.when(qc != mc)
                    def _():
                        start_from(given, given_p, given_q)

            @pl.when(jnp.logical_not(live))
            def _():
                src[b, pl.ds(s * rows, rows)] = jnp.zeros((rows, channels), BF)

        @pl.when(step == 0)
        def _():
            @pl.loop(0, nblocks)
            def _(b):
                for s in range(slots):
                    fetch(b, s)

            acc_in[...] = jnp.zeros_like(acc_in)
            acc_out[...] = jnp.zeros_like(acc_out)

        for j in range(per):
            b = step * per + j
            for s in range(slots):

                @pl.when(s < cnt_ref[b])
                def _():
                    pltpu.make_async_copy(owned.at[pl.ds(0, rows)], slot(b, s), sems.at[b, s]).wait()

        for j in range(per):
            b = step * per + j
            agg = dot(adj[j, 0], src[b, :rows], 1, 0)
            for s in range(1, slots):
                agg += dot(adj[j, s], src[b, s * rows : (s + 1) * rows], 1, 0)
            joined[j * rows : (j + 1) * rows, :channels] = agg.astype(BF)
        joined[:, channels:] = feat[...]
        x = joined[...]
        g = cot[...]
        pre = dot(x, win[...], 1, 0)
        gh = dot(g, wout[...], 1, 1)
        sg = 0.5 * jnp.tanh(0.5 * pre) + 0.5
        silu = pre * sg
        hidden = silu.astype(BF)
        gp = (gh * (sg + silu * (1.0 - sg))).astype(BF)
        gp_out[...] = gp
        acc_in[...] += dot(x, gp, 0, 0)
        acc_out[...] += dot(hidden, g, 0, 0)

        @pl.when(step == steps - 1)
        def _():
            for i in range(NX * NZ):
                for ref, c in ((keep, mc), (send, 1 - mc)):
                    x = (i // NZ + mx) & 3
                    at = pl.multiple_of(((x * NZ + i % NZ) * NC + c) * 8, 8)
                    ref[i, :, :hid] = acc_in[pl.ds(at, 8), :] * scale
                    ref[i, :, hid:] = acc_out[pl.ds(at, 8), :] * scale

    smem = pl.BlockSpec(memory_space=pltpu.SMEM)
    whole = pl.BlockSpec(memory_space=pl.ANY)
    fixed = lambda a: pl.BlockSpec(a.shape, lambda i: (0,) * a.ndim, pipeline_mode=pl.Buffered(1))
    tiled = pl.BlockSpec((tile, channels), lambda i: (i, 0))
    part = (NX * NZ, 8, hid + channels)
    return pl.pallas_call(
        kernel,
        grid=(steps,),
        out_shape=[
            jax.ShapeDtypeStruct((nodes, hid), BF),
            jax.ShapeDtypeStruct(part, F32),
            jax.ShapeDtypeStruct(part, F32),
        ],
        in_specs=[smem] * 4
        + [whole] * 7
        + [pl.BlockSpec((per, slots, rows, rows), lambda i: (i, 0, 0, 0)), tiled, tiled, fixed(weight_in), fixed(weight_out)],
        out_specs=[
            pl.BlockSpec((tile, hid), lambda i: (i, 0)),
            pl.BlockSpec(part, lambda i: (0, 0, 0)),
            pl.BlockSpec(part, lambda i: (0, 0, 0)),
        ],
        scratch_shapes=[
            pltpu.VMEM((nblocks, slots * rows, channels), BF),
            pltpu.VMEM((tile, 2 * channels), BF),
            pltpu.VMEM((2 * channels, hid), F32),
            pltpu.VMEM((hid, channels), F32),
            pltpu.SemaphoreType.DMA((nblocks, slots)),
        ],
        name="forward",
    )(neighbor, counts, wanted, position, features, *blocks, adjacency, features, cotangent, weight_in, weight_out)


def backward(grad_preact, weight_in, adjacency, neighbor, counts):
    nblocks, slots, rows, _ = adjacency.shape
    nodes, hid = grad_preact.shape
    channels = weight_in.shape[0] // 2
    per = 4
    tile = per * rows
    steps = nblocks // per

    def kernel(nb_ref, cnt_ref, gp, win, adj, out, acc):
        step = pl.program_id(0)

        @pl.when(step == 0)
        def _():
            acc[...] = jnp.zeros_like(acc)

        gj = dot(gp[...], win[...], 1, 1)
        mine = pl.ds(pl.multiple_of(step * tile, tile), tile)
        acc[mine, :] = acc[mine, :] + gj[:, channels:]
        ga = gj[:, :channels].astype(BF)
        for j in range(per):
            b = step * per + j
            for s in range(slots):
                nb = nb_ref[b, s]

                @pl.when(jnp.logical_and(s < cnt_ref[b], nb < nblocks))
                def _():
                    at = pl.ds(pl.multiple_of(jnp.minimum(nb, nblocks - 1) * rows, rows), rows)
                    acc[at, :] = acc[at, :] + dot(adj[j, s], ga[j * rows : (j + 1) * rows], 0, 0)

        @pl.when(step == steps - 1)
        def _():
            out[...] = acc[...].astype(BF)

    smem = pl.BlockSpec(memory_space=pltpu.SMEM)
    return pl.pallas_call(
        kernel,
        grid=(steps,),
        out_shape=jax.ShapeDtypeStruct((nodes, channels), BF),
        in_specs=[
            smem,
            smem,
            pl.BlockSpec((tile, hid), lambda i: (i, 0)),
            pl.BlockSpec(weight_in.shape, lambda i: (0, 0), pipeline_mode=pl.Buffered(1)),
            pl.BlockSpec((per, slots, rows, rows), lambda i: (i, 0, 0, 0)),
        ],
        out_specs=pl.BlockSpec((nodes, channels), lambda i: (0, 0)),
        scratch_shapes=[pltpu.VMEM((nodes, channels), F32)],
        name="backward",
        cost_estimate=pl.CostEstimate(
            flops=2 * nodes * (2 * hid * channels + slots * rows * channels),
            bytes_accessed=2 * nodes * (hid + 3 * channels),
            transcendentals=0,
        ),
    )(neighbor, counts, grad_preact, weight_in, adjacency)


def reduce_terms(keep, send, hid):
    keep = (keep + move(send, dc=1)).reshape(NX, NZ, *keep.shape[1:])
    there = keep[1:].astype(WIRE)
    parts = []
    for k in (1, 3, 2):
        parts.append(move(there[k - 1], dx=k))
    keep = (keep[0] + parts[0].astype(F32) + parts[1].astype(F32) + parts[2].astype(F32)).astype(WIRE)
    columns = [[place(x, z, c) for z in range(NZ)] for x in range(NX) for c in range(NC)]
    keep = lax.all_to_all(keep, "dom", 0, 0, axis_index_groups=columns).astype(F32).sum(0)
    a, b, c = (lax.ppermute(keep, "grp", [(i, i ^ k) for i in range(4)]) for k in (1, 2, 3))
    at = slice(0, hid), slice(hid, None)
    return [(keep[:, i] + a[:, i]) + (b[:, i] + c[:, i]) for i in at]


def layer(
    features, boundary_cache, adjacency, neighbor, counts, wanted, weight_in, weight_out, cotangent
):
    block_rows = adjacency.shape[2]
    channels = features.shape[1]
    hid = weight_in.shape[1]
    at = lax.axis_index("dom")
    position = jnp.stack([at // (NZ * NC), at // NC % NZ, at % NC]).astype(jnp.int32)
    exported = boundary_cache.astype(BF).reshape(-1, block_rows, channels)
    other = move(wanted, dc=1)
    near, far = gather_plane(exported)
    (given,) = pick(near, (other,), position)
    given = move(given, dc=1)
    (kept,) = pick(near, (wanted,), position)
    node_total = features.shape[0] * lax.axis_size("grp") * lax.axis_size("dom")
    scale = 1.0 / math.sqrt(node_total)
    grad_preact, keep, send = forward(
        features, (kept, given, *far), adjacency, cotangent, weight_in, weight_out,
        neighbor, counts, wanted, position, scale,
    )
    grad_features = backward(grad_preact, weight_in, adjacency, neighbor, counts)
    total = reduce_terms(keep, send, hid)
    return (grad_features, *total)


def solution(mesh):
    in_specs = (
        P(("grp", "dom"), None),
        P(("grp", "dom"), None),
        P(("grp", "dom"), None, None, None),
        P(("grp", "dom"), None),
        P(("grp", "dom")),
        P(("grp", "dom"), None),
        P(),
        P(),
        P(("grp", "dom"), None),
    )
    out_specs = (P(("grp", "dom"), None), P("dom", None), P("dom", None))
    return jax.shard_map(layer, mesh=mesh, in_specs=in_specs, out_specs=out_specs, check_vma=False)
```

profile of v0, /device:TPU:2, one launch (start us, length us, event | category | flops | bytes accessed | tf_op | source)
XLA Modules:
  0.0 122.3 jit_solution(3410454607774722253)
XLA Ops:
  0.6 1.0 convert_element_type.20
  1.6 2.3 %collective-permute-start = (bf16[2,128,256]{2,1,0:T(8,128)(2,1)S(1)}, bf16[2,128,256]{2,1,0:T(8,128)(2,1)S(1)}, u32[]{:S(2)}, u32[]{:S(2)}) collective-permute-start(bf16[2,128,256]{2,1,0:T(8,128)(2,1)S(1)} %bitcast.4), channel_id=1, source_target_pairs={{0,48},{1,49},{2,50},{3,51},{4,52},{5,53},{6,54},{7,55},{8,56},{9,... | collective-permute-start | bytes 393224 | tf_op jit(solution)/shard_map/ppermute | solution.py:25
  3.9 0.0 collective-permute-start.1
  3.9 3.1 %collective-permute-start.2 = (bf16[2,128,256]{2,1,0:T(8,128)(2,1)S(1)}, bf16[2,128,256]{2,1,0:T(8,128)(2,1)S(1)}, u32[]{:S(2)}, u32[]{:S(2)}) collective-permute-start(bf16[2,128,256]{2,1,0:T(8,128)(2,1)S(1)} %bitcast.6), channel_id=1, source_target_pairs={{0,32},{1,33},{2,34},{3,35},{4,36},{5,37},{6,38},{7,39},{8,40},{9,... | collective-permute-start | bytes 393224 | tf_op jit(solution)/shard_map/ppermute | solution.py:25
  7.0 0.0 collective-permute-done
  7.1 0.0 copy-start
  7.1 5.9 %collective-permute-start.4 = (bf16[4,128,256]{2,1,0:T(8,128)(2,1)S(1)}, bf16[4,128,256]{2,1,0:T(8,128)(2,1)S(1)}, u32[]{:S(2)}, u32[]{:S(2)}) collective-permute-start(bf16[4,128,256]{2,1,0:T(8,128)(2,1)S(1)} %pad_maximum_fusion.refs_2_), channel_id=1, source_target_pairs={{0,14},{1,15},{2,0},{3,1},{4,2},{5,3},{6,4},{7,5},{8,6},{9,7},{10,... | collective-permute-start | bytes 786440 | tf_op jit(solution)/shard_map/ppermute | solution.py:25
  13.0 0.0 collective-permute-start.3
  13.0 0.0 collective-permute-done.1
  13.0 0.0 collective-permute-done.2
  13.1 3.5 %collective-permute-start.6 = (bf16[4,128,256]{2,1,0:T(8,128)(2,1)S(1)}, bf16[4,128,256]{2,1,0:T(8,128)(2,1)S(1)}, u32[]{:S(2)}, u32[]{:S(2)}) collective-permute-start(bf16[4,128,256]{2,1,0:T(8,128)(2,1)S(1)} %constant_dynamic-update-slice_fusion.refs_3_), channel_id=1, source_target_pairs={{0,14},{1,15},{2,0},{3,1},{4,2},{5,3},{6,4},{7,5},{8,6},{9,7},{10,... | collective-permute-start | bytes 786440 | tf_op jit(solution)/shard_map/ppermute | solution.py:25
  16.6 0.0 collective-permute-start.5
  16.6 3.0 %collective-permute-done.4.refs_5_ = bf16[4,128,256]{2,1,0:T(8,128)(2,1)S(1)} collective-permute-done((bf16[4,128,256]{2,1,0:T(8,128)(2,1)S(1)}, bf16[4,128,256]{2,1,0:T(8,128)(2,1)S(1)}, u32[]{:S(2)}, u32[]{:S(2)}) %collective-permute-start.4) | collective-permute-done | bytes 262176 | tf_op jit(solution)/shard_map/ppermute | solution.py:25
  19.6 3.7 %collective-permute-start.8 = (bf16[4,128,256]{2,1,0:T(8,128)(2,1)S(1)}, bf16[4,128,256]{2,1,0:T(8,128)(2,1)S(1)}, u32[]{:S(2)}, u32[]{:S(2)}) collective-permute-start(bf16[4,128,256]{2,1,0:T(8,128)(2,1)S(1)} %collective-permute-done.4.refs_5_), channel_id=1, source_target_pairs={{0,14},{1,15},{2,0},{3,1},{4,2},{5,3},{6,4},{7,5},{8,6},{9,7},{10,... | collective-permute-start | bytes 786440 | tf_op jit(solution)/shard_map/ppermute | solution.py:25
  23.3 0.0 collective-permute-done.3.refs_4_
  23.3 0.0 collective-permute-start.7
  23.3 1.9 %collective-permute-done.6.refs_7_ = bf16[4,128,256]{2,1,0:T(8,128)(2,1)S(1)} collective-permute-done((bf16[4,128,256]{2,1,0:T(8,128)(2,1)S(1)}, bf16[4,128,256]{2,1,0:T(8,128)(2,1)S(1)}, u32[]{:S(2)}, u32[]{:S(2)}) %collective-permute-start.6) | collective-permute-done | bytes 262176 | tf_op jit(solution)/shard_map/ppermute | solution.py:25
  25.2 3.7 %collective-permute-start.10 = (bf16[4,128,256]{2,1,0:T(8,128)(2,1)S(1)}, bf16[4,128,256]{2,1,0:T(8,128)(2,1)S(1)}, u32[]{:S(2)}, u32[]{:S(2)}) collective-permute-start(bf16[4,128,256]{2,1,0:T(8,128)(2,1)S(1)} %collective-permute-done.6.refs_7_), channel_id=1, source_target_pairs={{0,14},{1,15},{2,0},{3,1},{4,2},{5,3},{6,4},{7,5},{8,6},{9,7},{10,... | collective-permute-start | bytes 786440 | tf_op jit(solution)/shard_map/ppermute | solution.py:25
  28.9 0.0 collective-permute-done.5.refs_6_
  28.9 0.0 collective-permute-start.9
  28.9 1.9 %collective-permute-done.8.refs_9_ = bf16[4,128,256]{2,1,0:T(8,128)(2,1)S(1)} collective-permute-done((bf16[4,128,256]{2,1,0:T(8,128)(2,1)S(1)}, bf16[4,128,256]{2,1,0:T(8,128)(2,1)S(1)}, u32[]{:S(2)}, u32[]{:S(2)}) %collective-permute-start.8) | collective-permute-done | bytes 262176 | tf_op jit(solution)/shard_map/ppermute | solution.py:25
  30.8 3.7 %collective-permute-start.12 = (bf16[4,128,256]{2,1,0:T(8,128)(2,1)S(1)}, bf16[4,128,256]{2,1,0:T(8,128)(2,1)S(1)}, u32[]{:S(2)}, u32[]{:S(2)}) collective-permute-start(bf16[4,128,256]{2,1,0:T(8,128)(2,1)S(1)} %collective-permute-done.8.refs_9_), channel_id=1, source_target_pairs={{0,14},{1,15},{2,0},{3,1},{4,2},{5,3},{6,4},{7,5},{8,6},{9,7},{10,... | collective-permute-start | bytes 786440 | tf_op jit(solution)/shard_map/ppermute | solution.py:25
  34.5 1.9 %collective-permute-done.10.refs_11_ = bf16[4,128,256]{2,1,0:T(8,128)(2,1)S(1)} collective-permute-done((bf16[4,128,256]{2,1,0:T(8,128)(2,1)S(1)}, bf16[4,128,256]{2,1,0:T(8,128)(2,1)S(1)}, u32[]{:S(2)}, u32[]{:S(2)}) %collective-permute-start.10) | collective-permute-done | bytes 262176 | tf_op jit(solution)/shard_map/ppermute | solution.py:25
  36.4 3.7 %collective-permute-start.14 = (bf16[4,128,256]{2,1,0:T(8,128)(2,1)S(1)}, bf16[4,128,256]{2,1,0:T(8,128)(2,1)S(1)}, u32[]{:S(2)}, u32[]{:S(2)}) collective-permute-start(bf16[4,128,256]{2,1,0:T(8,128)(2,1)S(1)} %collective-permute-done.10.refs_11_), channel_id=1, source_target_pairs={{0,14},{1,15},{2,0},{3,1},{4,2},{5,3},{6,4},{7,5},{8,6},{9,7},{10,... | collective-permute-start | bytes 786440 | tf_op jit(solution)/shard_map/ppermute | solution.py:25
  40.1 0.0 collective-permute-done.9.refs_10_
  40.1 0.0 collective-permute-start.13
  40.1 0.3 collective-permute-start.15
  40.5 0.7 pad_add_fusion.refs_1_.at_ref
  41.1 0.6 collective-permute-done.15.refs_0_
  41.7 0.3 collective-permute-done.12.refs_13_
  42.1 3.4 %collective-permute-done.11.refs_12_ = bf16[4,128,256]{2,1,0:T(8,128)(2,1)S(1)} collective-permute-done((bf16[4,128,256]{2,1,0:T(8,128)(2,1)S(1)}, bf16[4,128,256]{2,1,0:T(8,128)(2,1)S(1)}, u32[]{:S(2)}, u32[]{:S(2)}) %collective-permute-start.11) | collective-permute-done | bytes 262176 | tf_op jit(solution)/shard_map/ppermute | solution.py:25
  45.5 0.4 collective-permute-done.14.refs_15_
  45.8 3.5 %collective-permute-done.13.refs_14_ = bf16[4,128,256]{2,1,0:T(8,128)(2,1)} collective-permute-done((bf16[4,128,256]{2,1,0:T(8,128)(2,1)S(1)}, bf16[4,128,256]{2,1,0:T(8,128)(2,1)}, u32[]{:S(2)}, u32[]{:S(2)}) %collective-permute-start.13) | collective-permute-done | bytes 262176 | tf_op jit(solution)/shard_map/ppermute | solution.py:25
  49.5 3.4 %pick.3 = bf16[28,128,256]{2,1,0:T(8,128)(2,1)} custom-call(s32[1,64]{1,0:T(1,128)} %copy-done.19, s32[3]{0:T(128)} %pad_add_fusion.refs_1_.at_ref, bf16[4,128,256]{2,1,0:T(8,128)(2,1)} %copy-done, bf16[4,128,256]{2,1,0:T(8,128)(2,1)} %copy-done.2, bf16[4,128,256]{2,1,0:T(8,128)(2,1)} %copy-done.4, bf16[4,128,256]{2,1,0:T(8,128)(2,1)} %copy-done.3, ...), custom_call_target="tpu_custom_call" | custom-call | tf_op jit(solution)/shard_map/pick/pallas_call | solution.py:98
  52.9 0.1 collective-permute-start.16
  53.0 0.1 collective-permute-start.17
  53.1 3.2 %collective-permute-start.18 = (bf16[4,128,256]{2,1,0:T(8,128)(2,1)}, bf16[4,128,256]{2,1,0:T(8,128)(2,1)S(1)}, u32[]{:S(2)}, u32[]{:S(2)}) collective-permute-start(bf16[4,128,256]{2,1,0:T(8,128)(2,1)} %copy-done.13), channel_id=1, source_target_pairs={{0,14},{1,15},{2,0},{3,1},{4,2},{5,3},{6,4},{7,5},{8,6},{9,7},{10,... | collective-permute-start | bytes 786440 | tf_op jit(solution)/shard_map/ppermute | solution.py:25
  56.3 6.8 %collective-permute-done.17.p4 = bf16[4,128,256]{2,1,0:T(8,128)(2,1)S(1)} collective-permute-done((bf16[4,128,256]{2,1,0:T(8,128)(2,1)}, bf16[4,128,256]{2,1,0:T(8,128)(2,1)S(1)}, u32[]{:S(2)}, u32[]{:S(2)}) %collective-permute-start.17) | collective-permute-done | bytes 262176 | tf_op jit(solution)/shard_map/ppermute | solution.py:25
  63.1 0.0 collective-permute-start.19
  63.1 0.5 collective-permute-start.20
  63.6 0.7 copy.13.nb_ref
  64.3 3.4 %pick.2.kept = bf16[28,128,256]{2,1,0:T(8,128)(2,1)} custom-call(s32[1,64]{1,0:T(1,128)} %want_ref.1, s32[3]{0:T(128)} %pad_add_fusion.refs_1_.at_ref, bf16[4,128,256]{2,1,0:T(8,128)(2,1)} %copy-done, bf16[4,128,256]{2,1,0:T(8,128)(2,1)} %copy-done.2, bf16[4,128,256]{2,1,0:T(8,128)(2,1)} %copy-done.4, bf16[4,128,256]{2,1,0:T(8,128)(2,1)} %copy-done.3, ...), custom_call_target="tpu_custom_call" | custom-call | tf_op jit(solution)/shard_map/pick/pallas_call | solution.py:98
  67.7 0.0 collective-permute-done.19.given_p
  67.8 0.7 copy-done.16
  68.4 0.1 copy-done.17
  68.6 1.2 %copy-done.1 = bf16[28,128,256]{2,1,0:T(8,128)(2,1)} copy-done((bf16[28,128,256]{2,1,0:T(8,128)(2,1)}, bf16[28,128,256]{2,1,0:T(8,128)(2,1)S(1)}, u32[]{:S(2)}) %copy-start.1) | copy-done | bytes 1835032
  69.8 12.3 %forward.1 = (bf16[3072,512]{1,0:T(8,128)(2,1)}, f32[32,8,768]{2,1,0:T(8,128)}, f32[32,8,768]{2,1,0:T(8,128)}) custom-call(s32[24,2]{1,0:T(8,128)} %copy.13.nb_ref, s32[24]{0:T(128)} %cnt_ref.3, s32[1,64]{1,0:T(1,128)} %want_ref.1, s32[3]{0:T(128)} %pad_add_fusion.refs_1_.at_ref, bf16[3072,256]{1,0:T(8,128)(2,1)} %feat.1, bf16[28,128,256]{2,1,0:T(8,128)(2,1)} %pick.2.kept, ...), custom_call_target="tpu_custom_call" | custom-call | tf_op jit(solution)/shard_map/forward/pallas_call | solution.py:237
  82.2 0.1 collective-permute-start.21
  82.3 2.5 %collective-permute-done.21 = f32[32,8,768]{2,1,0:T(8,128)S(1)} collective-permute-done((f32[32,8,768]{2,1,0:T(8,128)}, f32[32,8,768]{2,1,0:T(8,128)S(1)}, u32[]{:S(2)}, u32[]{:S(2)}) %collective-permute-start.21) | collective-permute-done | bytes 786464 | tf_op jit(solution)/shard_map/ppermute | solution.py:25
  84.7 1.2 %fusion.5 = (bf16[32,8,768]{2,1,0:T(8,128)(2,1)S(1)}, f32[32,8,768]{2,1,0:T(8,128)S(1)}) fusion(f32[32,8,768]{2,1,0:T(8,128)} %get-tuple-element.7, f32[32,8,768]{2,1,0:T(8,128)S(1)} %collective-permute-done.21), kind=kLoop, calls=%fused_computation.15 | loop fusion | flops 393216 | bytes 2752512 | tf_op jit(solution)/shard_map/convert
  86.0 1.5 %collective-permute-start.22 = (bf16[8,8,768]{2,1,0:T(8,128)(2,1)S(1)}, bf16[8,8,768]{2,1,0:T(8,128)(2,1)S(1)}, u32[]{:S(2)}, u32[]{:S(2)}) collective-permute-start(bf16[8,8,768]{2,1,0:T(8,128)(2,1)S(1)} %get-tuple-element.11), channel_id=1, source_target_pairs={{0,16},{1,17},{2,18},{3,19},{4,20},{5,21},{6,22},{7,23},{8,24},{9,... | collective-permute-start | bytes 294920 | tf_op jit(solution)/shard_map/ppermute | solution.py:25
  87.5 2.0 %collective-permute-start.24 = (bf16[8,8,768]{2,1,0:T(8,128)(2,1)S(1)}, bf16[8,8,768]{2,1,0:T(8,128)(2,1)S(1)}, u32[]{:S(2)}, u32[]{:S(2)}) collective-permute-start(bf16[8,8,768]{2,1,0:T(8,128)(2,1)S(1)} %get-tuple-element.12), channel_id=1, source_target_pairs={{0,32},{1,33},{2,34},{3,35},{4,36},{5,37},{6,38},{7,39},{8,40},{9,... | collective-permute-start | bytes 294920 | tf_op jit(solution)/shard_map/ppermute | solution.py:25
  89.5 2.2 %collective-permute-start.23 = (bf16[8,8,768]{2,1,0:T(8,128)(2,1)S(1)}, bf16[8,8,768]{2,1,0:T(8,128)(2,1)S(1)}, u32[]{:S(2)}, u32[]{:S(2)}) collective-permute-start(bf16[8,8,768]{2,1,0:T(8,128)(2,1)S(1)} %get-tuple-element.13), channel_id=1, source_target_pairs={{0,48},{1,49},{2,50},{3,51},{4,52},{5,53},{6,54},{7,55},{8,56},{9,... | collective-permute-start | bytes 294920 | tf_op jit(solution)/shard_map/ppermute | solution.py:25
  91.8 2.9 %collective-permute-done.24 = bf16[8,8,768]{2,1,0:T(8,128)(2,1)S(1)} collective-permute-done((bf16[8,8,768]{2,1,0:T(8,128)(2,1)S(1)}, bf16[8,8,768]{2,1,0:T(8,128)(2,1)S(1)}, u32[]{:S(2)}, u32[]{:S(2)}) %collective-permute-start.24) | collective-permute-done | bytes 98336 | tf_op jit(solution)/shard_map/ppermute | solution.py:25
  94.6 1.1 collective-permute-done.23
  95.7 0.1 fusion.2
  95.7 12.6 %all_to_all.5 = bf16[8,8,768]{2,1,0:T(8,128)(2,1)S(1)} all-to-all(bf16[8,8,768]{2,1,0:T(8,128)(2,1)S(1)} %fusion.2), channel_id=1, replica_groups={{0,2,4,6,8,10,12,14},{1,3,5,7,9,11,13,15},{16,18,20,22,24,26,28,30},{17..., dimensions={0} | all-to-all | bytes 196608 | tf_op jit(solution)/shard_map/all_to_all | solution.py:328
  108.4 3.2 %collective-permute-start.27 = (f32[8,768]{1,0:T(8,128)S(1)}, f32[8,768]{1,0:T(8,128)S(1)}, u32[]{:S(2)}, u32[]{:S(2)}) collective-permute-start(f32[8,768]{1,0:T(8,128)S(1)} %convert_reduce_fusion), channel_id=1, source_target_pairs={{0,192},{64,128},{128,64},{192,0},{1,193},{65,129},{129,65},{193,1... | collective-permute-start | bytes 73736 | tf_op jit(solution)/shard_map/ppermute | solution.py:329
  111.6 0.6 collective-permute-start.26
  112.2 0.4 collective-permute-start.25
  112.5 8.5 %backward.1 = bf16[3072,256]{1,0:T(8,128)(2,1)} custom-call(s32[24,2]{1,0:T(8,128)} %copy.13.nb_ref, s32[24]{0:T(128)} %cnt_ref.3, bf16[3072,512]{1,0:T(8,128)(2,1)} %get-tuple-element.6.gp, bf16[512,512]{1,0:T(8,128)(2,1)} %win.3, bf16[24,2,128,128]{3,2,1,0:T(8,128)(2,1)} %adj.3), custom_call_target="tpu_custom_call" | custom-call | flops 2013265920 | bytes 7864320 | tf_op jit(solution)/shard_map/backward/pallas_call | solution.py:298
  121.0 0.0 collective-permute-done.25
  121.0 0.6 fusion.4
  121.6 0.6 fusion.3
  (49 shorter events, 0.2 us)
Async XLA Ops:
  1.6 5.4 %collective-permute-start = (bf16[2,128,256]{2,1,0:T(8,128)(2,1)S(1)}, bf16[2,128,256]{2,1,0:T(8,128)(2,1)S(1)}, u32[]{:S(2)}, u32[]{:S(2)}) collective-permute-start(bf16[2,128,256]{2,1,0:T(8,128)(2,1)S(1)} %bitcast.4), channel_id=1, source_target_pairs={{0,48},{1,49},{2,50},{3,51},{4,52},{5,53},{6,54},{7,55},{8,56},{9,... | collective-permute-start | bytes 393224 | tf_op jit(solution)/shard_map/ppermute | solution.py:25
  3.9 9.1 %collective-permute-start.1 = (bf16[2,128,256]{2,1,0:T(8,128)(2,1)S(1)}, bf16[2,128,256]{2,1,0:T(8,128)(2,1)S(1)}, u32[]{:S(2)}, u32[]{:S(2)}) collective-permute-start(bf16[2,128,256]{2,1,0:T(8,128)(2,1)S(1)} %bitcast.5), channel_id=1, source_target_pairs={{0,16},{1,17},{2,18},{3,19},{4,20},{5,21},{6,22},{7,23},{8,24},{9,... | collective-permute-start | bytes 393224 | tf_op jit(solution)/shard_map/ppermute | solution.py:25
  3.9 9.1 %collective-permute-start.2 = (bf16[2,128,256]{2,1,0:T(8,128)(2,1)S(1)}, bf16[2,128,256]{2,1,0:T(8,128)(2,1)S(1)}, u32[]{:S(2)}, u32[]{:S(2)}) collective-permute-start(bf16[2,128,256]{2,1,0:T(8,128)(2,1)S(1)} %bitcast.6), channel_id=1, source_target_pairs={{0,32},{1,33},{2,34},{3,35},{4,36},{5,37},{6,38},{7,39},{8,40},{9,... | collective-permute-start | bytes 393224 | tf_op jit(solution)/shard_map/ppermute | solution.py:25
  7.1 42.3 %copy-start = (bf16[4,128,256]{2,1,0:T(8,128)(2,1)}, bf16[4,128,256]{2,1,0:T(8,128)(2,1)S(1)}, u32[]{:S(2)}) copy-start(bf16[4,128,256]{2,1,0:T(8,128)(2,1)S(1)} %pad_maximum_fusion.refs_2_) | copy-start | bytes 786436
  7.1 12.5 %collective-permute-start.4 = (bf16[4,128,256]{2,1,0:T(8,128)(2,1)S(1)}, bf16[4,128,256]{2,1,0:T(8,128)(2,1)S(1)}, u32[]{:S(2)}, u32[]{:S(2)}) collective-permute-start(bf16[4,128,256]{2,1,0:T(8,128)(2,1)S(1)} %pad_maximum_fusion.refs_2_), channel_id=1, source_target_pairs={{0,14},{1,15},{2,0},{3,1},{4,2},{5,3},{6,4},{7,5},{8,6},{9,7},{10,... | collective-permute-start | bytes 786440 | tf_op jit(solution)/shard_map/ppermute | solution.py:25
  13.0 10.3 %collective-permute-start.3 = (bf16[4,128,256]{2,1,0:T(8,128)(2,1)S(1)}, bf16[4,128,256]{2,1,0:T(8,128)(2,1)S(1)}, u32[]{:S(2)}, u32[]{:S(2)}) collective-permute-start(bf16[4,128,256]{2,1,0:T(8,128)(2,1)S(1)} %pad_maximum_fusion.refs_2_), channel_id=1, source_target_pairs={{0,2},{1,3},{2,4},{3,5},{4,6},{5,7},{6,8},{7,9},{8,10},{9,11},{10,... | collective-permute-start | bytes 786440 | tf_op jit(solution)/shard_map/ppermute | solution.py:25
  13.1 36.3 %copy-start.2 = (bf16[4,128,256]{2,1,0:T(8,128)(2,1)}, bf16[4,128,256]{2,1,0:T(8,128)(2,1)S(1)}, u32[]{:S(2)}) copy-start(bf16[4,128,256]{2,1,0:T(8,128)(2,1)S(1)} %constant_dynamic-update-slice_fusion.refs_3_) | copy-start | bytes 786436
  13.1 12.1 %collective-permute-start.6 = (bf16[4,128,256]{2,1,0:T(8,128)(2,1)S(1)}, bf16[4,128,256]{2,1,0:T(8,128)(2,1)S(1)}, u32[]{:S(2)}, u32[]{:S(2)}) collective-permute-start(bf16[4,128,256]{2,1,0:T(8,128)(2,1)S(1)} %constant_dynamic-update-slice_fusion.refs_3_), channel_id=1, source_target_pairs={{0,14},{1,15},{2,0},{3,1},{4,2},{5,3},{6,4},{7,5},{8,6},{9,7},{10,... | collective-permute-start | bytes 786440 | tf_op jit(solution)/shard_map/ppermute | solution.py:25
  16.6 12.3 %collective-permute-start.5 = (bf16[4,128,256]{2,1,0:T(8,128)(2,1)S(1)}, bf16[4,128,256]{2,1,0:T(8,128)(2,1)S(1)}, u32[]{:S(2)}, u32[]{:S(2)}) collective-permute-start(bf16[4,128,256]{2,1,0:T(8,128)(2,1)S(1)} %constant_dynamic-update-slice_fusion.refs_3_), channel_id=1, source_target_pairs={{0,2},{1,3},{2,4},{3,5},{4,6},{5,7},{6,8},{7,9},{8,10},{9,11},{10,... | collective-permute-start | bytes 786440 | tf_op jit(solution)/shard_map/ppermute | solution.py:25
  19.6 29.8 %copy-start.3 = (bf16[4,128,256]{2,1,0:T(8,128)(2,1)}, bf16[4,128,256]{2,1,0:T(8,128)(2,1)S(1)}, u32[]{:S(2)}) copy-start(bf16[4,128,256]{2,1,0:T(8,128)(2,1)S(1)} %collective-permute-done.4.refs_5_) | copy-start | bytes 786436
  19.6 11.2 %collective-permute-start.8 = (bf16[4,128,256]{2,1,0:T(8,128)(2,1)S(1)}, bf16[4,128,256]{2,1,0:T(8,128)(2,1)S(1)}, u32[]{:S(2)}, u32[]{:S(2)}) collective-permute-start(bf16[4,128,256]{2,1,0:T(8,128)(2,1)S(1)} %collective-permute-done.4.refs_5_), channel_id=1, source_target_pairs={{0,14},{1,15},{2,0},{3,1},{4,2},{5,3},{6,4},{7,5},{8,6},{9,7},{10,... | collective-permute-start | bytes 786440 | tf_op jit(solution)/shard_map/ppermute | solution.py:25
  23.3 26.1 %copy-start.4 = (bf16[4,128,256]{2,1,0:T(8,128)(2,1)}, bf16[4,128,256]{2,1,0:T(8,128)(2,1)S(1)}, u32[]{:S(2)}) copy-start(bf16[4,128,256]{2,1,0:T(8,128)(2,1)S(1)} %collective-permute-done.3.refs_4_) | copy-start | bytes 786436
  23.3 11.2 %collective-permute-start.7 = (bf16[4,128,256]{2,1,0:T(8,128)(2,1)S(1)}, bf16[4,128,256]{2,1,0:T(8,128)(2,1)S(1)}, u32[]{:S(2)}, u32[]{:S(2)}) collective-permute-start(bf16[4,128,256]{2,1,0:T(8,128)(2,1)S(1)} %collective-permute-done.3.refs_4_), channel_id=1, source_target_pairs={{0,2},{1,3},{2,4},{3,5},{4,6},{5,7},{6,8},{7,9},{8,10},{9,11},{10,... | collective-permute-start | bytes 786440 | tf_op jit(solution)/shard_map/ppermute | solution.py:25
  25.2 24.2 %copy-start.5 = (bf16[4,128,256]{2,1,0:T(8,128)(2,1)}, bf16[4,128,256]{2,1,0:T(8,128)(2,1)S(1)}, u32[]{:S(2)}) copy-start(bf16[4,128,256]{2,1,0:T(8,128)(2,1)S(1)} %collective-permute-done.6.refs_7_) | copy-start | bytes 786436
  25.2 11.2 %collective-permute-start.10 = (bf16[4,128,256]{2,1,0:T(8,128)(2,1)S(1)}, bf16[4,128,256]{2,1,0:T(8,128)(2,1)S(1)}, u32[]{:S(2)}, u32[]{:S(2)}) collective-permute-start(bf16[4,128,256]{2,1,0:T(8,128)(2,1)S(1)} %collective-permute-done.6.refs_7_), channel_id=1, source_target_pairs={{0,14},{1,15},{2,0},{3,1},{4,2},{5,3},{6,4},{7,5},{8,6},{9,7},{10,... | collective-permute-start | bytes 786440 | tf_op jit(solution)/shard_map/ppermute | solution.py:25
  28.9 20.5 %copy-start.6 = (bf16[4,128,256]{2,1,0:T(8,128)(2,1)}, bf16[4,128,256]{2,1,0:T(8,128)(2,1)S(1)}, u32[]{:S(2)}) copy-start(bf16[4,128,256]{2,1,0:T(8,128)(2,1)S(1)} %collective-permute-done.5.refs_6_) | copy-start | bytes 786436
  28.9 11.2 %collective-permute-start.9 = (bf16[4,128,256]{2,1,0:T(8,128)(2,1)S(1)}, bf16[4,128,256]{2,1,0:T(8,128)(2,1)S(1)}, u32[]{:S(2)}, u32[]{:S(2)}) collective-permute-start(bf16[4,128,256]{2,1,0:T(8,128)(2,1)S(1)} %collective-permute-done.5.refs_6_), channel_id=1, source_target_pairs={{0,2},{1,3},{2,4},{3,5},{4,6},{5,7},{6,8},{7,9},{8,10},{9,11},{10,... | collective-permute-start | bytes 786440 | tf_op jit(solution)/shard_map/ppermute | solution.py:25
  30.8 18.6 %copy-start.7 = (bf16[4,128,256]{2,1,0:T(8,128)(2,1)}, bf16[4,128,256]{2,1,0:T(8,128)(2,1)S(1)}, u32[]{:S(2)}) copy-start(bf16[4,128,256]{2,1,0:T(8,128)(2,1)S(1)} %collective-permute-done.8.refs_9_) | copy-start | bytes 786436
  30.8 11.2 %collective-permute-start.12 = (bf16[4,128,256]{2,1,0:T(8,128)(2,1)S(1)}, bf16[4,128,256]{2,1,0:T(8,128)(2,1)S(1)}, u32[]{:S(2)}, u32[]{:S(2)}) collective-permute-start(bf16[4,128,256]{2,1,0:T(8,128)(2,1)S(1)} %collective-permute-done.8.refs_9_), channel_id=1, source_target_pairs={{0,14},{1,15},{2,0},{3,1},{4,2},{5,3},{6,4},{7,5},{8,6},{9,7},{10,... | collective-permute-start | bytes 786440 | tf_op jit(solution)/shard_map/ppermute | solution.py:25
  34.5 14.9 %copy-start.8 = (bf16[4,128,256]{2,1,0:T(8,128)(2,1)}, bf16[4,128,256]{2,1,0:T(8,128)(2,1)S(1)}, u32[]{:S(2)}) copy-start(bf16[4,128,256]{2,1,0:T(8,128)(2,1)S(1)} %collective-permute-done.7.refs_8_) | copy-start | bytes 786436
  34.5 10.9 %collective-permute-start.11 = (bf16[4,128,256]{2,1,0:T(8,128)(2,1)S(1)}, bf16[4,128,256]{2,1,0:T(8,128)(2,1)S(1)}, u32[]{:S(2)}, u32[]{:S(2)}) collective-permute-start(bf16[4,128,256]{2,1,0:T(8,128)(2,1)S(1)} %collective-permute-done.7.refs_8_), channel_id=1, source_target_pairs={{0,2},{1,3},{2,4},{3,5},{4,6},{5,7},{6,8},{7,9},{8,10},{9,11},{10,... | collective-permute-start | bytes 786440 | tf_op jit(solution)/shard_map/ppermute | solution.py:25
  36.4 13.0 %copy-start.9 = (bf16[4,128,256]{2,1,0:T(8,128)(2,1)}, bf16[4,128,256]{2,1,0:T(8,128)(2,1)S(1)}, u32[]{:S(2)}) copy-start(bf16[4,128,256]{2,1,0:T(8,128)(2,1)S(1)} %collective-permute-done.10.refs_11_) | copy-start | bytes 786436
  36.4 9.4 %collective-permute-start.14 = (bf16[4,128,256]{2,1,0:T(8,128)(2,1)S(1)}, bf16[4,128,256]{2,1,0:T(8,128)(2,1)S(1)}, u32[]{:S(2)}, u32[]{:S(2)}) collective-permute-start(bf16[4,128,256]{2,1,0:T(8,128)(2,1)S(1)} %collective-permute-done.10.refs_11_), channel_id=1, source_target_pairs={{0,14},{1,15},{2,0},{3,1},{4,2},{5,3},{6,4},{7,5},{8,6},{9,7},{10,... | collective-permute-start | bytes 786440 | tf_op jit(solution)/shard_map/ppermute | solution.py:25
  40.1 9.3 %copy-start.10 = (bf16[4,128,256]{2,1,0:T(8,128)(2,1)}, bf16[4,128,256]{2,1,0:T(8,128)(2,1)S(1)}, u32[]{:S(2)}) copy-start(bf16[4,128,256]{2,1,0:T(8,128)(2,1)S(1)} %collective-permute-done.9.refs_10_) | copy-start | bytes 786436
  40.1 9.2 %collective-permute-start.13 = (bf16[4,128,256]{2,1,0:T(8,128)(2,1)S(1)}, bf16[4,128,256]{2,1,0:T(8,128)(2,1)}, u32[]{:S(2)}, u32[]{:S(2)}) collective-permute-start(bf16[4,128,256]{2,1,0:T(8,128)(2,1)S(1)} %collective-permute-done.9.refs_10_), channel_id=1, source_target_pairs={{0,2},{1,3},{2,4},{3,5},{4,6},{5,7},{6,8},{7,9},{8,10},{9,11},{10,... | collective-permute-start | bytes 786440 | tf_op jit(solution)/shard_map/ppermute | solution.py:25
  40.1 1.6 %collective-permute-start.15 = (s32[1,64]{1,0:T(1,128)}, s32[1,64]{1,0:T(1,128)S(1)}, u32[]{:S(2)}, u32[]{:S(2)}) collective-permute-start(s32[1,64]{1,0:T(1,128)} %want_ref.1), channel_id=1, source_target_pairs={{0,1},{1,0},{2,3},{3,2},{4,5},{5,4},{6,7},{7,6},{8,9},{9,8},{10,11... | collective-permute-start | bytes 776 | tf_op jit(solution)/shard_map/ppermute | solution.py:25
  41.1 22.5 %copy-start.18 = (s32[24,2]{0,1:T(2,128)S(1)}, s32[24,2]{0,1:T(2,128)}, u32[]{:S(2)}) copy-start(s32[24,2]{0,1:T(2,128)} %param.12) | copy-start | bytes 580
  41.7 7.7 %copy-start.19 = (s32[1,64]{1,0:T(1,128)}, s32[1,64]{1,0:T(1,128)S(1)}, u32[]{:S(2)}) copy-start(s32[1,64]{1,0:T(1,128)S(1)} %collective-permute-done.15.refs_0_) | copy-start | bytes 772
  42.0 7.4 %copy-start.11 = (bf16[4,128,256]{2,1,0:T(8,128)(2,1)}, bf16[4,128,256]{2,1,0:T(8,128)(2,1)S(1)}, u32[]{:S(2)}) copy-start(bf16[4,128,256]{2,1,0:T(8,128)(2,1)S(1)} %collective-permute-done.12.refs_13_) | copy-start | bytes 786436
  45.5 4.0 %copy-start.12 = (bf16[4,128,256]{2,1,0:T(8,128)(2,1)}, bf16[4,128,256]{2,1,0:T(8,128)(2,1)S(1)}, u32[]{:S(2)}) copy-start(bf16[4,128,256]{2,1,0:T(8,128)(2,1)S(1)} %collective-permute-done.11.refs_12_) | copy-start | bytes 786436
  45.8 3.6 %copy-start.13 = (bf16[4,128,256]{2,1,0:T(8,128)(2,1)}, bf16[4,128,256]{2,1,0:T(8,128)(2,1)S(1)}, u32[]{:S(2)}) copy-start(bf16[4,128,256]{2,1,0:T(8,128)(2,1)S(1)} %collective-permute-done.14.refs_15_) | copy-start | bytes 786436
  52.9 14.9 %collective-permute-start.16 = (bf16[28,128,256]{2,1,0:T(8,128)(2,1)}, bf16[28,128,256]{2,1,0:T(8,128)(2,1)S(1)}, u32[]{:S(2)}, u32[]{:S(2)}) collective-permute-start(bf16[28,128,256]{2,1,0:T(8,128)(2,1)} %pick.3), channel_id=1, source_target_pairs={{0,1},{1,0},{2,3},{3,2},{4,5},{5,4},{6,7},{7,6},{8,9},{9,8},{10,11... | collective-permute-start | bytes 5505032 | tf_op jit(solution)/shard_map/ppermute | solution.py:25
  53.0 10.1 %collective-permute-start.17 = (bf16[4,128,256]{2,1,0:T(8,128)(2,1)}, bf16[4,128,256]{2,1,0:T(8,128)(2,1)S(1)}, u32[]{:S(2)}, u32[]{:S(2)}) collective-permute-start(bf16[4,128,256]{2,1,0:T(8,128)(2,1)} %copy-done.12), channel_id=1, source_target_pairs={{0,2},{1,3},{2,4},{3,5},{4,6},{5,7},{6,8},{7,9},{8,10},{9,11},{10,... | collective-permute-start | bytes 786440 | tf_op jit(solution)/shard_map/ppermute | solution.py:25
  53.1 10.0 %collective-permute-start.18 = (bf16[4,128,256]{2,1,0:T(8,128)(2,1)}, bf16[4,128,256]{2,1,0:T(8,128)(2,1)S(1)}, u32[]{:S(2)}, u32[]{:S(2)}) collective-permute-start(bf16[4,128,256]{2,1,0:T(8,128)(2,1)} %copy-done.13), channel_id=1, source_target_pairs={{0,14},{1,15},{2,0},{3,1},{4,2},{5,3},{6,4},{7,5},{8,6},{9,7},{10,... | collective-permute-start | bytes 786440 | tf_op jit(solution)/shard_map/ppermute | solution.py:25
  63.1 4.6 %copy-start.14 = (bf16[4,128,256]{2,1,0:T(8,128)(2,1)}, bf16[4,128,256]{2,1,0:T(8,128)(2,1)S(1)}, u32[]{:S(2)}) copy-start(bf16[4,128,256]{2,1,0:T(8,128)(2,1)S(1)} %collective-permute-done.17.p4) | copy-start | bytes 786436
  63.1 4.6 %collective-permute-start.19 = (bf16[4,128,256]{2,1,0:T(8,128)(2,1)S(1)}, bf16[4,128,256]{2,1,0:T(8,128)(2,1)S(1)}, u32[]{:S(2)}, u32[]{:S(2)}) collective-permute-start(bf16[4,128,256]{2,1,0:T(8,128)(2,1)S(1)} %collective-permute-done.17.p4), channel_id=1, source_target_pairs={{0,1},{1,0},{2,3},{3,2},{4,5},{5,4},{6,7},{7,6},{8,9},{9,8},{10,11... | collective-permute-start | bytes 786440 | tf_op jit(solution)/shard_map/ppermute | solution.py:25
  63.1 4.6 %copy-start.15 = (bf16[4,128,256]{2,1,0:T(8,128)(2,1)}, bf16[4,128,256]{2,1,0:T(8,128)(2,1)S(1)}, u32[]{:S(2)}) copy-start(bf16[4,128,256]{2,1,0:T(8,128)(2,1)S(1)} %collective-permute-done.18.q4) | copy-start | bytes 786436
  63.1 4.6 %collective-permute-start.20 = (bf16[4,128,256]{2,1,0:T(8,128)(2,1)S(1)}, bf16[4,128,256]{2,1,0:T(8,128)(2,1)S(1)}, u32[]{:S(2)}, u32[]{:S(2)}) collective-permute-start(bf16[4,128,256]{2,1,0:T(8,128)(2,1)S(1)} %collective-permute-done.18.q4), channel_id=1, source_target_pairs={{0,1},{1,0},{2,3},{3,2},{4,5},{5,4},{6,7},{7,6},{8,9},{9,8},{10,11... | collective-permute-start | bytes 786440 | tf_op jit(solution)/shard_map/ppermute | solution.py:25
  67.7 0.7 copy-start.16
  67.7 0.8 copy-start.17
  68.6 1.2 %copy-start.1 = (bf16[28,128,256]{2,1,0:T(8,128)(2,1)}, bf16[28,128,256]{2,1,0:T(8,128)(2,1)S(1)}, u32[]{:S(2)}) copy-start(bf16[28,128,256]{2,1,0:T(8,128)(2,1)S(1)} %collective-permute-done.16.given) | copy-start | bytes 5505028
  82.2 2.6 %collective-permute-start.21 = (f32[32,8,768]{2,1,0:T(8,128)}, f32[32,8,768]{2,1,0:T(8,128)S(1)}, u32[]{:S(2)}, u32[]{:S(2)}) collective-permute-start(f32[32,8,768]{2,1,0:T(8,128)} %get-tuple-element.8), channel_id=1, source_target_pairs={{0,1},{1,0},{2,3},{3,2},{4,5},{5,4},{6,7},{7,6},{8,9},{9,8},{10,11... | collective-permute-start | bytes 2359304 | tf_op jit(solution)/shard_map/ppermute | solution.py:25
  86.0 5.8 %collective-permute-start.22 = (bf16[8,8,768]{2,1,0:T(8,128)(2,1)S(1)}, bf16[8,8,768]{2,1,0:T(8,128)(2,1)S(1)}, u32[]{:S(2)}, u32[]{:S(2)}) collective-permute-start(bf16[8,8,768]{2,1,0:T(8,128)(2,1)S(1)} %get-tuple-element.11), channel_id=1, source_target_pairs={{0,16},{1,17},{2,18},{3,19},{4,20},{5,21},{6,22},{7,23},{8,24},{9,... | collective-permute-start | bytes 294920 | tf_op jit(solution)/shard_map/ppermute | solution.py:25
  87.5 7.1 %collective-permute-start.24 = (bf16[8,8,768]{2,1,0:T(8,128)(2,1)S(1)}, bf16[8,8,768]{2,1,0:T(8,128)(2,1)S(1)}, u32[]{:S(2)}, u32[]{:S(2)}) collective-permute-start(bf16[8,8,768]{2,1,0:T(8,128)(2,1)S(1)} %get-tuple-element.12), channel_id=1, source_target_pairs={{0,32},{1,33},{2,34},{3,35},{4,36},{5,37},{6,38},{7,39},{8,40},{9,... | collective-permute-start | bytes 294920 | tf_op jit(solution)/shard_map/ppermute | solution.py:25
  89.5 6.1 %collective-permute-start.23 = (bf16[8,8,768]{2,1,0:T(8,128)(2,1)S(1)}, bf16[8,8,768]{2,1,0:T(8,128)(2,1)S(1)}, u32[]{:S(2)}, u32[]{:S(2)}) collective-permute-start(bf16[8,8,768]{2,1,0:T(8,128)(2,1)S(1)} %get-tuple-element.13), channel_id=1, source_target_pairs={{0,48},{1,49},{2,50},{3,51},{4,52},{5,53},{6,54},{7,55},{8,56},{9,... | collective-permute-start | bytes 294920 | tf_op jit(solution)/shard_map/ppermute | solution.py:25
  108.4 12.7 %collective-permute-start.27 = (f32[8,768]{1,0:T(8,128)S(1)}, f32[8,768]{1,0:T(8,128)S(1)}, u32[]{:S(2)}, u32[]{:S(2)}) collective-permute-start(f32[8,768]{1,0:T(8,128)S(1)} %convert_reduce_fusion), channel_id=1, source_target_pairs={{0,192},{64,128},{128,64},{192,0},{1,193},{65,129},{129,65},{193,1... | collective-permute-start | bytes 73736 | tf_op jit(solution)/shard_map/ppermute | solution.py:329
  111.6 9.5 %collective-permute-start.26 = (f32[8,768]{1,0:T(8,128)S(1)}, f32[8,768]{1,0:T(8,128)S(1)}, u32[]{:S(2)}, u32[]{:S(2)}) collective-permute-start(f32[8,768]{1,0:T(8,128)S(1)} %convert_reduce_fusion), channel_id=1, source_target_pairs={{0,128},{64,192},{128,0},{192,64},{1,129},{65,193},{129,1},{193,65... | collective-permute-start | bytes 73736 | tf_op jit(solution)/shard_map/ppermute | solution.py:329
  112.2 8.9 %collective-permute-start.25 = (f32[8,768]{1,0:T(8,128)S(1)}, f32[8,768]{1,0:T(8,128)S(1)}, u32[]{:S(2)}, u32[]{:S(2)}) collective-permute-start(f32[8,768]{1,0:T(8,128)S(1)} %convert_reduce_fusion), channel_id=1, source_target_pairs={{0,64},{64,0},{128,192},{192,128},{1,65},{65,1},{129,193},{193,129... | collective-permute-start | bytes 73736 | tf_op jit(solution)/shard_map/ppermute | solution.py:329
where the time goes:
time: 124 us; the launch traced here: 122 us
  starting transfers between devices  43.9 us (35%)
  waiting for transfers between devices  30.2 us (24%)
  Pallas kernels  27.6 us (22%)
  blocking collectives  12.6 us (10%)
  other arithmetic  4.17 us (3%)
  local copies, waits for them, and re-layouts  2.86 us (2%)
    ppermute x25, starting transfers between devices, move(): return lax.ppermute(a, 'dom', pairs)  39.7 us
    ppermute x25, waiting for transfers between devices, move(): return lax.ppermute(a, 'dom', pairs)  30.2 us
    all_to_all x1, blocking collectives, reduce_terms(): lax.all_to_all(keep, 'dom', 0, 0, axis_index_groups=columns).astype(F32)  12.6 us
    pallas_call x1, Pallas kernels, forward(): pl.pallas_call(kernel, grid=(steps,), out_shape=[jax.ShapeDtypeStruct((no...  12.3 us
    pallas_call x1, Pallas kernels, backward(): pl.pallas_call(kernel, grid=(steps,), out_shape=jax.ShapeDtypeStruct((nod...  8.49 us
    pallas_call x2, Pallas kernels, pick(): pl.pallas_call(kernel, out_shape=[jax.ShapeDtypeStruct((count, *block), B...  6.77 us
    ppermute x3, starting transfers between devices, reduce_terms(): lax.ppermute(keep, 'grp', [(i, i ^ k) for i in range(4)])  4.18 us
    unnamed x42, local copies, waits for them, and re-layouts  2.83 us
  transfers between devices with their start and end apart: 28, of which 13 were waited for; matrix products, arithmetic and copies ran while one was open for 1% of the time, Pallas kernels for 10%

commit v1 on v0

--- a/solution.py
+++ b/solution.py
@@ -42,7 +42,7 @@
 
 
 def gather_plane(own):
-    near = Table()
+    near, first, third = Table(), Table(), Table()
 
     def go(a, **step):
         return move(a, **step)
@@ -50,21 +50,21 @@
     c1, c2, c3 = go(own, dx=1), go(own, dx=-1), go(own, dx=2)
     p, q = jnp.concatenate([own, c2]), jnp.concatenate([c1, c3])
     px, qx = (0, 1), (-1, 2)
-    near.add(p, px, 0)
-    near.add(q, qx, 0)
+    for a, xs in ((p, px), (q, qx)):
+        near.add(a, xs, 0)
+        first.add(a, xs, 0)
     pp, pm, qp, qm = p, p, q, q
     for k in (1, 2, 3):
         pp, pm = go(pp, dz=1), go(pm, dz=-1)
         qp, qm = go(qp, dz=1), go(qm, dz=-1)
-        near.add(pp, px, -k)
-        near.add(pm, px, k)
-        near.add(qp, qx, -k)
-        near.add(qm, qx, k)
+        for a, xs, dz in ((pp, px, -k), (pm, px, k), (qp, qx, -k), (qm, qx, k)):
+            near.add(a, xs, dz)
+            (first if k < 3 else third).add(a, xs, dz)
     p4 = go(pp, dz=1)
     given_p = move(p4, dc=1)
     q4 = go(qm, dz=-1)
     given_q = move(q4, dc=1)
-    return near, (p4, q4, given_p, given_q)
+    return near, first, third, (p4, q4, given_p, given_q)
 
 
 def pick(table, wants, position):
@@ -123,11 +123,13 @@
     per = PER
     tile = per * rows
     steps = nblocks // per
+    parts = len(blocks) - 4
 
     def kernel(
-        nb_ref, cnt_ref, want_ref, at_ref, owned, kept, given, p4, q4, given_p, given_q, adj, feat, cot, win, wout,
-        gp_out, keep, send, src, joined, acc_in, acc_out, sems,
+        nb_ref, cnt_ref, want_ref, at_ref, owned, given, given_third, given_p, given_q, *refs
     ):
+        pieces = refs[:parts]
+        adj, feat, cot, win, wout, gp_out, keep, send, src, joined, acc_in, acc_out, sems = refs[parts:]
         step = pl.program_id(0)
         mx, mz, mc = at_ref[0], at_ref[1], at_ref[2]
 
@@ -142,26 +144,47 @@
             qx, qz, qc = q >> 4, (q >> 1) & 7, q & 1
             dx, dz = (qx - mx) & 3, (qz - mz) & 7
             far = dz == 4
-            rel = dx * 7 + jnp.where(dz > 4, dz - 1, jnp.minimum(dz, 3))
             e = want_ref[0, q]
 
             def start(ref):
                 pltpu.make_async_copy(ref, slot(b, s), sems.at[b, s]).start()
 
-            def start_from(table, tp, tq):
-                @pl.when(jnp.logical_not(far))
-                def _():
-                    start(table.at[rel])
-
-                @pl.when(far)
-                def _():
-                    @pl.when(dx < 2)
-                    def _():
-                        start(tp.at[2 * dx + e])
-
-                    @pl.when(dx >= 2)
-                    def _():
-                        start(tq.at[2 * (3 - dx) + e])
+            inner = dx < 2
+            at = jnp.where(inner, 2 * dx, 2 * (3 - dx)) + e
+            hop = jnp.minimum(dz, NZ - dz)
+            side = jnp.where(inner, 0, 2) + jnp.where(dz < 4, 1, 0)
+            piece = jnp.where(inner, 0, 1) + jnp.where(hop == 0, 0, 4 * hop - 2 + jnp.where(far, 0, side - jnp.where(inner, 0, 1)))
+
+            def start_piece(low, high):
+                if high - low == 1:
+                    start(pieces[low].at[at])
+                    return
+                mid = (low + high) // 2
+
+                @pl.when(piece < mid)
+                def _():
+                    start_piece(low, mid)
+
+                @pl.when(piece >= mid)
+                def _():
+                    start_piece(mid, high)
+
+            def start_given():
+                @pl.when(hop < 3)
+                def _():
+                    start(given.at[dx * 5 + jnp.where(dz < 3, dz, dz - 3)])
+
+                @pl.when(hop == 3)
+                def _():
+                    start(given_third.at[dx * 2 + jnp.where(dz == 3, 0, 1)])
+
+                @pl.when(jnp.logical_and(far, inner))
+                def _():
+                    start(given_p.at[at])
+
+                @pl.when(jnp.logical_and(far, jnp.logical_not(inner)))
+                def _():
+                    start(given_q.at[at])
 
             @pl.when(live)
             def _():
@@ -173,11 +196,11 @@
                 def _():
                     @pl.when(qc == mc)
                     def _():
-                        start_from(kept, p4, q4)
+                        start_piece(0, parts)
 
                     @pl.when(qc != mc)
                     def _():
-                        start_from(given, given_p, given_q)
+                        start_given()
 
             @pl.when(jnp.logical_not(live))
             def _():
@@ -243,7 +266,7 @@
             jax.ShapeDtypeStruct(part, F32),
         ],
         in_specs=[smem] * 4
-        + [whole] * 7
+        + [whole] * (5 + parts)
         + [pl.BlockSpec((per, slots, rows, rows), lambda i: (i, 0, 0, 0)), tiled, tiled, fixed(weight_in), fixed(weight_out)],
         out_specs=[
             pl.BlockSpec((tile, hid), lambda i: (i, 0)),
@@ -261,25 +284,47 @@
     )(neighbor, counts, wanted, position, features, *blocks, adjacency, features, cotangent, weight_in, weight_out)
 
 
-def backward(grad_preact, weight_in, adjacency, neighbor, counts):
-    nblocks, slots, rows, _ = adjacency.shape
+def join_gradient(grad_preact, weight_in, half, before=()):
     nodes, hid = grad_preact.shape
     channels = weight_in.shape[0] // 2
-    per = 4
-    tile = per * rows
+    tile = nodes // 4
+
+    def kernel(gp, win, *refs):
+        ga, right = refs[-2:]
+        gj = dot(gp[...], win[...], 1, 1)
+        ga[...] = gj[:, :channels].astype(BF)
+        right[...] = gj[:, channels:]
+
+    return pl.pallas_call(
+        kernel,
+        grid=(2,),
+        out_shape=[jax.ShapeDtypeStruct((nodes, channels), t) for t in (BF, F32)],
+        in_specs=[
+            pl.BlockSpec((tile, hid), lambda i: (i + 2 * half, 0)),
+            pl.BlockSpec(weight_in.shape, lambda i: (0, 0), pipeline_mode=pl.Buffered(1)),
+        ]
+        + [pl.BlockSpec(memory_space=pl.ANY)] * len(before),
+        out_specs=[pl.BlockSpec((tile, channels), lambda i: (i + 2 * half, 0))] * 2,
+        input_output_aliases={2 + i: i for i in range(len(before))},
+        name="joingrad",
+    )(grad_preact, weight_in, *before)
+
+
+def scatter_gradient(grad_aggregate, right, adjacency, neighbor, counts):
+    nblocks, slots, rows, _ = adjacency.shape
+    nodes, channels = right.shape
+    per = PER
     steps = nblocks // per
 
-    def kernel(nb_ref, cnt_ref, gp, win, adj, out, acc):
+    def kernel(nb_ref, cnt_ref, right_ref, ga, adj, out, acc, base, sem):
         step = pl.program_id(0)
+        fill = pltpu.make_async_copy(right_ref, base, sem)
 
         @pl.when(step == 0)
         def _():
+            fill.start()
             acc[...] = jnp.zeros_like(acc)
 
-        gj = dot(gp[...], win[...], 1, 1)
-        mine = pl.ds(pl.multiple_of(step * tile, tile), tile)
-        acc[mine, :] = acc[mine, :] + gj[:, channels:]
-        ga = gj[:, :channels].astype(BF)
         for j in range(per):
             b = step * per + j
             for s in range(slots):
@@ -292,7 +337,8 @@
 
         @pl.when(step == steps - 1)
         def _():
-            out[...] = acc[...].astype(BF)
+            fill.wait()
+            out[...] = (acc[...] + base[...]).astype(BF)
 
     smem = pl.BlockSpec(memory_space=pltpu.SMEM)
     return pl.pallas_call(
@@ -302,23 +348,23 @@
         in_specs=[
             smem,
             smem,
-            pl.BlockSpec((tile, hid), lambda i: (i, 0)),
-            pl.BlockSpec(weight_in.shape, lambda i: (0, 0), pipeline_mode=pl.Buffered(1)),
+            pl.BlockSpec(memory_space=pl.ANY),
+            pl.BlockSpec((per * rows, channels), lambda i: (i, 0)),
             pl.BlockSpec((per, slots, rows, rows), lambda i: (i, 0, 0, 0)),
         ],
         out_specs=pl.BlockSpec((nodes, channels), lambda i: (0, 0)),
-        scratch_shapes=[pltpu.VMEM((nodes, channels), F32)],
-        name="backward",
-        cost_estimate=pl.CostEstimate(
-            flops=2 * nodes * (2 * hid * channels + slots * rows * channels),
-            bytes_accessed=2 * nodes * (hid + 3 * channels),
-            transcendentals=0,
-        ),
-    )(neighbor, counts, grad_preact, weight_in, adjacency)
+        scratch_shapes=[
+            pltpu.VMEM((nodes, channels), F32),
+            pltpu.VMEM((nodes, channels), F32),
+            pltpu.SemaphoreType.DMA(()),
+        ],
+        name="scattergrad",
+    )(neighbor, counts, right, grad_aggregate, adjacency)
 
 
 def reduce_terms(keep, send, hid):
-    keep = (keep + move(send, dc=1)).reshape(NX, NZ, *keep.shape[1:])
+    send = move(send, dc=1)
+    keep = (keep + send).reshape(NX, NZ, *keep.shape[1:])
     there = keep[1:].astype(WIRE)
     parts = []
     for k in (1, 3, 2):
@@ -326,7 +372,10 @@
     keep = (keep[0] + parts[0].astype(F32) + parts[1].astype(F32) + parts[2].astype(F32)).astype(WIRE)
     columns = [[place(x, z, c) for z in range(NZ)] for x in range(NX) for c in range(NC)]
     keep = lax.all_to_all(keep, "dom", 0, 0, axis_index_groups=columns).astype(F32).sum(0)
-    a, b, c = (lax.ppermute(keep, "grp", [(i, i ^ k) for i in range(4)]) for k in (1, 2, 3))
+    parts = []
+    for k in (1, 2, 3):
+        parts.append(lax.ppermute(keep, "grp", [(i, i ^ k) for i in range(4)]))
+    a, b, c = parts
     at = slice(0, hid), slice(hid, None)
     return [(keep[:, i] + a[:, i]) + (b[:, i] + c[:, i]) for i in at]
 
@@ -341,17 +390,20 @@
     position = jnp.stack([at // (NZ * NC), at // NC % NZ, at % NC]).astype(jnp.int32)
     exported = boundary_cache.astype(BF).reshape(-1, block_rows, channels)
     other = move(wanted, dc=1)
-    near, far = gather_plane(exported)
-    (given,) = pick(near, (other,), position)
+    near, first, third, far = gather_plane(exported)
+    (given,) = pick(first, (other,), position)
     given = move(given, dc=1)
-    (kept,) = pick(near, (wanted,), position)
+    (given_third,) = pick(third, (other,), position)
+    given_third = move(given_third, dc=1)
     node_total = features.shape[0] * lax.axis_size("grp") * lax.axis_size("dom")
     scale = 1.0 / math.sqrt(node_total)
     grad_preact, keep, send = forward(
-        features, (kept, given, *far), adjacency, cotangent, weight_in, weight_out,
+        features, (given, given_third, *far[2:], *near.arrays, *far[:2]), adjacency, cotangent, weight_in, weight_out,
         neighbor, counts, wanted, position, scale,
     )
-    grad_features = backward(grad_preact, weight_in, adjacency, neighbor, counts)
+    joined = join_gradient(grad_preact, weight_in, 0)
+    grad_aggregate, right = join_gradient(grad_preact, weight_in, 1, joined)
+    grad_features = scatter_gradient(grad_aggregate, right, adjacency, neighbor, counts)
     total = reduce_terms(keep, send, hid)
     return (grad_features, *total)
 

time: 124 us -> 127 us (1.024)
  Pallas kernels: 27.6 us -> 31.3 us
  starting transfers between devices: 43.9 us -> 41.7 us
  local copies, waits for them, and re-layouts: 2.86 us -> 4.57 us
    pallas_call x1 -> x3, Pallas kernels: 8.49 us -> 13 us  [the longest x2 7.06 us: join_gradient(): pl.pallas_call(kernel, grid=(2,), out_shape=[jax.ShapeDtypeStruct((nodes,...]
    ppermute x25 -> x26, starting transfers between devices: 39.7 us -> 37.6 us  [move(): return lax.ppermute(a, 'dom', pairs)]
    unnamed x42 -> x46, local copies, waits for them, and re-layouts: 2.83 us -> 4.54 us
    pallas_call x2, Pallas kernels: 6.77 us -> 5.5 us  [pick(): pl.pallas_call(kernel, out_shape=[jax.ShapeDtypeStruct((count, *block), B...]
    ppermute x25 -> x26, waiting for transfers between devices: 30.2 us -> 29.5 us  [move(): return lax.ppermute(a, 'dom', pairs)]
  transfers between devices with their start and end apart: 28 -> 29, of which waited for: 13 -> 16; matrix products, arithmetic and copies ran while one was open for 1% -> 1% of each run, Pallas kernels for 10% -> 12%
where the time goes in v1:
time: 127 us; the launch traced here: 125 us
  starting transfers between devices  41.7 us (33%)
  Pallas kernels  31.3 us (25%)
  waiting for transfers between devices  29.5 us (23%)
  blocking collectives  12.9 us (10%)
  local copies, waits for them, and re-layouts  4.57 us (4%)
  other arithmetic  4.17 us (3%)
    ppermute x26, starting transfers between devices, move(): return lax.ppermute(a, 'dom', pairs)  37.6 us
    ppermute x26, waiting for transfers between devices, move(): return lax.ppermute(a, 'dom', pairs)  29.5 us
    all_to_all x1, blocking collectives, reduce_terms(): lax.all_to_all(keep, 'dom', 0, 0, axis_index_groups=columns).astype(F32)  12.9 us
    pallas_call x1, Pallas kernels, forward(): pl.pallas_call(kernel, grid=(steps,), out_shape=[jax.ShapeDtypeStruct((no...  12.8 us
    pallas_call x2, Pallas kernels, join_gradient(): pl.pallas_call(kernel, grid=(2,), out_shape=[jax.ShapeDtypeStruct((nodes,...  7.06 us
    pallas_call x1, Pallas kernels, scatter_gradient(): pl.pallas_call(kernel, grid=(steps,), out_shape=jax.ShapeDtypeStruct((nod...  5.96 us
    pallas_call x2, Pallas kernels, pick(): pl.pallas_call(kernel, out_shape=[jax.ShapeDtypeStruct((count, *block), B...  5.5 us
    unnamed x46, local copies, waits for them, and re-layouts  4.54 us
  transfers between devices with their start and end apart: 29, of which 16 were waited for; matrix products, arithmetic and copies ran while one was open for 1% of the time, Pallas kernels for 12%

profile of v1, /device:TPU:2, one launch (start us, length us, event | category | flops | bytes accessed | tf_op | source)
XLA Modules:
  0.0 125.2 jit_solution(12206044377292696205)
XLA Ops:
  0.6 1.0 convert_element_type.20
  1.6 2.3 %collective-permute-start.1 = (bf16[2,128,256]{2,1,0:T(8,128)(2,1)S(1)}, bf16[2,128,256]{2,1,0:T(8,128)(2,1)S(1)}, u32[]{:S(2)}, u32[]{:S(2)}) collective-permute-start(bf16[2,128,256]{2,1,0:T(8,128)(2,1)S(1)} %bitcast.4), channel_id=1, source_target_pairs={{0,48},{1,49},{2,50},{3,51},{4,52},{5,53},{6,54},{7,55},{8,56},{9,... | collective-permute-start | bytes 393224 | tf_op jit(solution)/shard_map/ppermute | solution.py:25
  3.9 3.1 %collective-permute-start.3 = (bf16[2,128,256]{2,1,0:T(8,128)(2,1)S(1)}, bf16[2,128,256]{2,1,0:T(8,128)(2,1)S(1)}, u32[]{:S(2)}, u32[]{:S(2)}) collective-permute-start(bf16[2,128,256]{2,1,0:T(8,128)(2,1)S(1)} %bitcast.6), channel_id=1, source_target_pairs={{0,32},{1,33},{2,34},{3,35},{4,36},{5,37},{6,38},{7,39},{8,40},{9,... | collective-permute-start | bytes 393224 | tf_op jit(solution)/shard_map/ppermute | solution.py:25
  7.1 5.9 %collective-permute-start.5 = (bf16[4,128,256]{2,1,0:T(8,128)(2,1)S(1)}, bf16[4,128,256]{2,1,0:T(8,128)(2,1)S(1)}, u32[]{:S(2)}, u32[]{:S(2)}) collective-permute-start(bf16[4,128,256]{2,1,0:T(8,128)(2,1)S(1)} %pad_maximum_fusion.refs_2_.refs_0_), channel_id=1, source_target_pairs={{0,14},{1,15},{2,0},{3,1},{4,2},{5,3},{6,4},{7,5},{8,6},{9,7},{10,... | collective-permute-start | bytes 786440 | tf_op jit(solution)/shard_map/ppermute | solution.py:25
  13.0 0.0 collective-permute-done.3
  13.1 3.5 %collective-permute-start.7 = (bf16[4,128,256]{2,1,0:T(8,128)(2,1)S(1)}, bf16[4,128,256]{2,1,0:T(8,128)(2,1)S(1)}, u32[]{:S(2)}, u32[]{:S(2)}) collective-permute-start(bf16[4,128,256]{2,1,0:T(8,128)(2,1)S(1)} %constant_dynamic-update-slice_fusion.refs_3_.refs_1_), channel_id=1, source_target_pairs={{0,14},{1,15},{2,0},{3,1},{4,2},{5,3},{6,4},{7,5},{8,6},{9,7},{10,... | collective-permute-start | bytes 786440 | tf_op jit(solution)/shard_map/ppermute | solution.py:25
  16.6 0.0 collective-permute-start.6
  16.6 3.0 %collective-permute-done.5.refs_5_.refs_3_ = bf16[4,128,256]{2,1,0:T(8,128)(2,1)S(1)} collective-permute-done((bf16[4,128,256]{2,1,0:T(8,128)(2,1)S(1)}, bf16[4,128,256]{2,1,0:T(8,128)(2,1)S(1)}, u32[]{:S(2)}, u32[]{:S(2)}) %collective-permute-start.5) | collective-permute-done | bytes 262176 | tf_op jit(solution)/shard_map/ppermute | solution.py:25
  19.6 3.7 %collective-permute-start.9 = (bf16[4,128,256]{2,1,0:T(8,128)(2,1)S(1)}, bf16[4,128,256]{2,1,0:T(8,128)(2,1)S(1)}, u32[]{:S(2)}, u32[]{:S(2)}) collective-permute-start(bf16[4,128,256]{2,1,0:T(8,128)(2,1)S(1)} %collective-permute-done.5.refs_5_.refs_3_), channel_id=1, source_target_pairs={{0,14},{1,15},{2,0},{3,1},{4,2},{5,3},{6,4},{7,5},{8,6},{9,7},{10,... | collective-permute-start | bytes 786440 | tf_op jit(solution)/shard_map/ppermute | solution.py:25
  23.3 1.9 %collective-permute-done.7.refs_7_.refs_5_ = bf16[4,128,256]{2,1,0:T(8,128)(2,1)S(1)} collective-permute-done((bf16[4,128,256]{2,1,0:T(8,128)(2,1)S(1)}, bf16[4,128,256]{2,1,0:T(8,128)(2,1)S(1)}, u32[]{:S(2)}, u32[]{:S(2)}) %collective-permute-start.7) | collective-permute-done | bytes 262176 | tf_op jit(solution)/shard_map/ppermute | solution.py:25
  25.2 3.7 %collective-permute-start.11 = (bf16[4,128,256]{2,1,0:T(8,128)(2,1)S(1)}, bf16[4,128,256]{2,1,0:T(8,128)(2,1)S(1)}, u32[]{:S(2)}, u32[]{:S(2)}) collective-permute-start(bf16[4,128,256]{2,1,0:T(8,128)(2,1)S(1)} %collective-permute-done.7.refs_7_.refs_5_), channel_id=1, source_target_pairs={{0,14},{1,15},{2,0},{3,1},{4,2},{5,3},{6,4},{7,5},{8,6},{9,7},{10,... | collective-permute-start | bytes 786440 | tf_op jit(solution)/shard_map/ppermute | solution.py:25
  28.9 0.0 collective-permute-done.6.refs_6_.refs_4_
  28.9 0.0 collective-permute-start.10
  28.9 0.1 collective-permute-start
  29.0 0.7 pad_add_fusion.refs_1_.at_ref
  29.7 0.6 collective-permute-done.refs_0_
  30.3 0.5 collective-permute-done.9.refs_9_.refs_7_
  30.8 3.4 %collective-permute-done.8.refs_8_.refs_6_ = bf16[4,128,256]{2,1,0:T(8,128)(2,1)S(1)} collective-permute-done((bf16[4,128,256]{2,1,0:T(8,128)(2,1)S(1)}, bf16[4,128,256]{2,1,0:T(8,128)(2,1)S(1)}, u32[]{:S(2)}, u32[]{:S(2)}) %collective-permute-start.8) | collective-permute-done | bytes 262176 | tf_op jit(solution)/shard_map/ppermute | solution.py:25
  34.2 0.4 collective-permute-done.11.refs_11_.refs_9_
  34.6 3.4 %collective-permute-done.10.refs_10_.refs_8_ = bf16[4,128,256]{2,1,0:T(8,128)(2,1)S(1)} collective-permute-done((bf16[4,128,256]{2,1,0:T(8,128)(2,1)S(1)}, bf16[4,128,256]{2,1,0:T(8,128)(2,1)S(1)}, u32[]{:S(2)}, u32[]{:S(2)}) %collective-permute-start.10) | collective-permute-done | bytes 262176 | tf_op jit(solution)/shard_map/ppermute | solution.py:25
  38.1 0.7 copy-done.10
  38.8 3.0 %pick.2 = bf16[20,128,256]{2,1,0:T(8,128)(2,1)} custom-call(s32[1,64]{1,0:T(1,128)} %copy-done.20, s32[3]{0:T(128)} %pad_add_fusion.refs_1_.at_ref, bf16[4,128,256]{2,1,0:T(8,128)(2,1)} %copy-done, bf16[4,128,256]{2,1,0:T(8,128)(2,1)} %copy-done.1, bf16[4,128,256]{2,1,0:T(8,128)(2,1)} %copy-done.4, bf16[4,128,256]{2,1,0:T(8,128)(2,1)} %copy-done.3, ...), custom_call_target="tpu_custom_call" | custom-call | tf_op jit(solution)/shard_map/pick/pallas_call | solution.py:98
  41.8 0.0 copy-start.21
  41.9 0.1 collective-permute-start.12
  42.0 0.1 collective-permute-start.13
  42.0 3.2 %collective-permute-start.16 = (bf16[4,128,256]{2,1,0:T(8,128)(2,1)}, bf16[4,128,256]{2,1,0:T(8,128)(2,1)S(1)}, u32[]{:S(2)}, u32[]{:S(2)}) collective-permute-start(bf16[4,128,256]{2,1,0:T(8,128)(2,1)} %copy-done.9), channel_id=1, source_target_pairs={{0,14},{1,15},{2,0},{3,1},{4,2},{5,3},{6,4},{7,5},{8,6},{9,7},{10,... | collective-permute-start | bytes 786440 | tf_op jit(solution)/shard_map/ppermute | solution.py:25
  45.3 0.0 collective-permute-start.14
  45.3 2.0 %collective-permute-start.15 = (bf16[4,128,256]{2,1,0:T(8,128)(2,1)}, bf16[4,128,256]{2,1,0:T(8,128)(2,1)S(1)}, u32[]{:S(2)}, u32[]{:S(2)}) collective-permute-start(bf16[4,128,256]{2,1,0:T(8,128)(2,1)} %copy-done.10), channel_id=1, source_target_pairs={{0,2},{1,3},{2,4},{3,5},{4,6},{5,7},{6,8},{7,9},{8,10},{9,11},{10,... | collective-permute-start | bytes 786440 | tf_op jit(solution)/shard_map/ppermute | solution.py:25
  47.3 5.3 %collective-permute-done.13.refs_2_.refs_10_ = bf16[4,128,256]{2,1,0:T(8,128)(2,1)S(1)} collective-permute-done((bf16[4,128,256]{2,1,0:T(8,128)(2,1)}, bf16[4,128,256]{2,1,0:T(8,128)(2,1)S(1)}, u32[]{:S(2)}, u32[]{:S(2)}) %collective-permute-start.13) | collective-permute-done | bytes 262176 | tf_op jit(solution)/shard_map/ppermute | solution.py:25
  52.7 3.2 %collective-permute-start.20 = (bf16[4,128,256]{2,1,0:T(8,128)(2,1)S(1)}, bf16[4,128,256]{2,1,0:T(8,128)(2,1)S(1)}, u32[]{:S(2)}, u32[]{:S(2)}) collective-permute-start(bf16[4,128,256]{2,1,0:T(8,128)(2,1)S(1)} %collective-permute-done.16.refs_5_.refs_13_), channel_id=1, source_target_pairs={{0,14},{1,15},{2,0},{3,1},{4,2},{5,3},{6,4},{7,5},{8,6},{9,7},{10,... | collective-permute-start | bytes 786440 | tf_op jit(solution)/shard_map/ppermute | solution.py:25
  55.9 2.0 %collective-permute-done.14.refs_3_.refs_11_ = bf16[4,128,256]{2,1,0:T(8,128)(2,1)S(1)} collective-permute-done((bf16[4,128,256]{2,1,0:T(8,128)(2,1)}, bf16[4,128,256]{2,1,0:T(8,128)(2,1)S(1)}, u32[]{:S(2)}, u32[]{:S(2)}) %collective-permute-start.14) | collective-permute-done | bytes 262176 | tf_op jit(solution)/shard_map/ppermute | solution.py:25
  57.9 0.3 collective-permute-done.15.refs_4_.refs_12_
  58.3 0.4 copy-done.13
  58.6 0.7 copy-done.14
  59.4 2.5 %pick.3 = bf16[8,128,256]{2,1,0:T(8,128)(2,1)} custom-call(s32[1,64]{1,0:T(1,128)} %copy-done.20, s32[3]{0:T(128)} %pad_add_fusion.refs_1_.at_ref, bf16[4,128,256]{2,1,0:T(8,128)(2,1)} %copy-done.11, bf16[4,128,256]{2,1,0:T(8,128)(2,1)} %copy-done.13, bf16[4,128,256]{2,1,0:T(8,128)(2,1)} %copy-done.14, bf16[4,128,256]{2,1,0:T(8,128)(2,1)} %copy-done.12), custom_call_target="tpu_custom_call" | custom-call | tf_op jit(solution)/shard_map/pick/pallas_call | solution.py:98
  61.9 0.1 collective-permute-start.17
  62.0 1.4 %collective-permute-done.18.refs_14_ = bf16[4,128,256]{2,1,0:T(8,128)(2,1)S(1)} collective-permute-done((bf16[4,128,256]{2,1,0:T(8,128)(2,1)S(1)}, bf16[4,128,256]{2,1,0:T(8,128)(2,1)S(1)}, u32[]{:S(2)}, u32[]{:S(2)}) %collective-permute-start.18) | collective-permute-done | bytes 262176 | tf_op jit(solution)/shard_map/ppermute | solution.py:25
  63.3 0.5 collective-permute-start.21
  63.8 0.7 copy.15.nb_ref
  64.5 0.3 collective-permute-done.19.given_p
  64.9 0.4 collective-permute-done.21.given_q
  65.3 0.3 copy-done.18
  65.6 0.4 copy-done.19
  65.9 0.2 copy-done.15
  66.2 1.1 copy-done.2
  67.2 12.8 %forward.1 = (bf16[3072,512]{1,0:T(8,128)(2,1)}, f32[32,8,768]{2,1,0:T(8,128)}, f32[32,8,768]{2,1,0:T(8,128)}) custom-call(s32[24,2]{1,0:T(8,128)} %copy.15.nb_ref, s32[24]{0:T(128)} %cnt_ref.3, s32[1,64]{1,0:T(1,128)} %want_ref.1, s32[3]{0:T(128)} %pad_add_fusion.refs_1_.at_ref, bf16[3072,256]{1,0:T(8,128)(2,1)} %refs_17_.1, ...), custom_call_target="tpu_custom_call" | custom-call | tf_op jit(solution)/shard_map/forward/pallas_call | solution.py:260
  80.0 0.1 collective-permute-start.22
  80.1 2.5 %collective-permute-done.22 = f32[32,8,768]{2,1,0:T(8,128)S(1)} collective-permute-done((f32[32,8,768]{2,1,0:T(8,128)}, f32[32,8,768]{2,1,0:T(8,128)S(1)}, u32[]{:S(2)}, u32[]{:S(2)}) %collective-permute-start.22) | collective-permute-done | bytes 786464 | tf_op jit(solution)/shard_map/ppermute | solution.py:25
  82.6 1.2 fusion.5
  83.8 1.5 %collective-permute-start.23 = (bf16[8,8,768]{2,1,0:T(8,128)(2,1)S(1)}, bf16[8,8,768]{2,1,0:T(8,128)(2,1)S(1)}, u32[]{:S(2)}, u32[]{:S(2)}) collective-permute-start(bf16[8,8,768]{2,1,0:T(8,128)(2,1)S(1)} %get-tuple-element.19), channel_id=1, source_target_pairs={{0,16},{1,17},{2,18},{3,19},{4,20},{5,21},{6,22},{7,23},{8,24},{9,... | collective-permute-start | bytes 294920 | tf_op jit(solution)/shard_map/ppermute | solution.py:25
  85.3 2.2 %collective-permute-start.25 = (bf16[8,8,768]{2,1,0:T(8,128)(2,1)S(1)}, bf16[8,8,768]{2,1,0:T(8,128)(2,1)S(1)}, u32[]{:S(2)}, u32[]{:S(2)}) collective-permute-start(bf16[8,8,768]{2,1,0:T(8,128)(2,1)S(1)} %get-tuple-element.20), channel_id=1, source_target_pairs={{0,32},{1,33},{2,34},{3,35},{4,36},{5,37},{6,38},{7,39},{8,40},{9,... | collective-permute-start | bytes 294920 | tf_op jit(solution)/shard_map/ppermute | solution.py:25
  87.5 2.2 %collective-permute-start.24 = (bf16[8,8,768]{2,1,0:T(8,128)(2,1)S(1)}, bf16[8,8,768]{2,1,0:T(8,128)(2,1)S(1)}, u32[]{:S(2)}, u32[]{:S(2)}) collective-permute-start(bf16[8,8,768]{2,1,0:T(8,128)(2,1)S(1)} %get-tuple-element.21), channel_id=1, source_target_pairs={{0,48},{1,49},{2,50},{3,51},{4,52},{5,53},{6,54},{7,55},{8,56},{9,... | collective-permute-start | bytes 294920 | tf_op jit(solution)/shard_map/ppermute | solution.py:25
  89.7 2.8 %collective-permute-done.25 = bf16[8,8,768]{2,1,0:T(8,128)(2,1)S(1)} collective-permute-done((bf16[8,8,768]{2,1,0:T(8,128)(2,1)S(1)}, bf16[8,8,768]{2,1,0:T(8,128)(2,1)S(1)}, u32[]{:S(2)}, u32[]{:S(2)}) %collective-permute-start.25) | collective-permute-done | bytes 98336 | tf_op jit(solution)/shard_map/ppermute | solution.py:25
  92.5 1.2 collective-permute-done.24
  93.7 0.1 fusion.2
  93.8 12.9 %all_to_all.5 = bf16[8,8,768]{2,1,0:T(8,128)(2,1)S(1)} all-to-all(bf16[8,8,768]{2,1,0:T(8,128)(2,1)S(1)} %fusion.2), channel_id=1, replica_groups={{0,2,4,6,8,10,12,14},{1,3,5,7,9,11,13,15},{16,18,20,22,24,26,28,30},{17..., dimensions={0} | all-to-all | bytes 196608 | tf_op jit(solution)/shard_map/all_to_all | solution.py:374
  106.7 3.0 %collective-permute-start.28 = (f32[8,768]{1,0:T(8,128)S(1)}, f32[8,768]{1,0:T(8,128)S(1)}, u32[]{:S(2)}, u32[]{:S(2)}) collective-permute-start(f32[8,768]{1,0:T(8,128)S(1)} %convert_reduce_fusion), channel_id=1, source_target_pairs={{0,192},{64,128},{128,64},{192,0},{1,193},{65,129},{129,65},{193,1... | collective-permute-start | bytes 73736 | tf_op jit(solution)/shard_map/ppermute | solution.py:377
  109.7 0.7 collective-permute-start.27
  110.5 0.4 collective-permute-start.26
  110.9 3.5 %joingrad.2 = (bf16[3072,256]{1,0:T(8,128)(2,1)}, f32[3072,256]{1,0:T(8,128)}) custom-call(bf16[3072,512]{1,0:T(8,128)(2,1)} %get-tuple-element.10.gp, bf16[512,512]{1,0:T(8,128)(2,1)} %win.3), custom_call_target="tpu_custom_call" | custom-call | tf_op jit(solution)/shard_map/joingrad/pallas_call | solution.py:298
  114.4 3.5 %joingrad.3 = (bf16[3072,256]{1,0:T(8,128)(2,1)}, f32[3072,256]{1,0:T(8,128)}) custom-call(bf16[3072,512]{1,0:T(8,128)(2,1)} %get-tuple-element.10.gp, bf16[512,512]{1,0:T(8,128)(2,1)} %win.3, bf16[3072,256]{1,0:T(8,128)(2,1)} %get-tuple-element.11.refs_0_, f32[3072,256]{1,0:T(8,128)} %get-tuple-element.12.refs_1_), custom_call_target="tpu_custom_call", output_to_operand_aliasing={{0}: (2, {}), {1}: (3, {})} | custom-call | tf_op jit(solution)/shard_map/joingrad/pallas_call | solution.py:298
  117.9 6.0 %scattergrad.1 = bf16[3072,256]{1,0:T(8,128)(2,1)} custom-call(s32[24,2]{1,0:T(8,128)} %copy.15.nb_ref, s32[24]{0:T(128)} %cnt_ref.3, f32[3072,256]{1,0:T(8,128)} %get-tuple-element.13.right_ref, bf16[3072,256]{1,0:T(8,128)(2,1)} %get-tuple-element.14.ga, bf16[24,2,128,128]{3,2,1,0:T(8,128)(2,1)} %adj.1), custom_call_target="tpu_custom_call" | custom-call | tf_op jit(solution)/shard_map/scattergrad/pallas_call | solution.py:344
  123.9 0.6 fusion.4
  124.5 0.6 fusion.3
  (57 shorter events, 0.2 us)
Async XLA Ops:
  1.6 5.4 %collective-permute-start.1 = (bf16[2,128,256]{2,1,0:T(8,128)(2,1)S(1)}, bf16[2,128,256]{2,1,0:T(8,128)(2,1)S(1)}, u32[]{:S(2)}, u32[]{:S(2)}) collective-permute-start(bf16[2,128,256]{2,1,0:T(8,128)(2,1)S(1)} %bitcast.4), channel_id=1, source_target_pairs={{0,48},{1,49},{2,50},{3,51},{4,52},{5,53},{6,54},{7,55},{8,56},{9,... | collective-permute-start | bytes 393224 | tf_op jit(solution)/shard_map/ppermute | solution.py:25
  3.9 9.1 %collective-permute-start.2 = (bf16[2,128,256]{2,1,0:T(8,128)(2,1)S(1)}, bf16[2,128,256]{2,1,0:T(8,128)(2,1)S(1)}, u32[]{:S(2)}, u32[]{:S(2)}) collective-permute-start(bf16[2,128,256]{2,1,0:T(8,128)(2,1)S(1)} %bitcast.5), channel_id=1, source_target_pairs={{0,16},{1,17},{2,18},{3,19},{4,20},{5,21},{6,22},{7,23},{8,24},{9,... | collective-permute-start | bytes 393224 | tf_op jit(solution)/shard_map/ppermute | solution.py:25
  3.9 9.1 %collective-permute-start.3 = (bf16[2,128,256]{2,1,0:T(8,128)(2,1)S(1)}, bf16[2,128,256]{2,1,0:T(8,128)(2,1)S(1)}, u32[]{:S(2)}, u32[]{:S(2)}) collective-permute-start(bf16[2,128,256]{2,1,0:T(8,128)(2,1)S(1)} %bitcast.6), channel_id=1, source_target_pairs={{0,32},{1,33},{2,34},{3,35},{4,36},{5,37},{6,38},{7,39},{8,40},{9,... | collective-permute-start | bytes 393224 | tf_op jit(solution)/shard_map/ppermute | solution.py:25
  7.1 30.9 %copy-start = (bf16[4,128,256]{2,1,0:T(8,128)(2,1)}, bf16[4,128,256]{2,1,0:T(8,128)(2,1)S(1)}, u32[]{:S(2)}) copy-start(bf16[4,128,256]{2,1,0:T(8,128)(2,1)S(1)} %pad_maximum_fusion.refs_2_.refs_0_) | copy-start | bytes 786436
  7.1 12.5 %collective-permute-start.5 = (bf16[4,128,256]{2,1,0:T(8,128)(2,1)S(1)}, bf16[4,128,256]{2,1,0:T(8,128)(2,1)S(1)}, u32[]{:S(2)}, u32[]{:S(2)}) collective-permute-start(bf16[4,128,256]{2,1,0:T(8,128)(2,1)S(1)} %pad_maximum_fusion.refs_2_.refs_0_), channel_id=1, source_target_pairs={{0,14},{1,15},{2,0},{3,1},{4,2},{5,3},{6,4},{7,5},{8,6},{9,7},{10,... | collective-permute-start | bytes 786440 | tf_op jit(solution)/shard_map/ppermute | solution.py:25
  13.0 10.3 %collective-permute-start.4 = (bf16[4,128,256]{2,1,0:T(8,128)(2,1)S(1)}, bf16[4,128,256]{2,1,0:T(8,128)(2,1)S(1)}, u32[]{:S(2)}, u32[]{:S(2)}) collective-permute-start(bf16[4,128,256]{2,1,0:T(8,128)(2,1)S(1)} %pad_maximum_fusion.refs_2_.refs_0_), channel_id=1, source_target_pairs={{0,2},{1,3},{2,4},{3,5},{4,6},{5,7},{6,8},{7,9},{8,10},{9,11},{10,... | collective-permute-start | bytes 786440 | tf_op jit(solution)/shard_map/ppermute | solution.py:25
  13.1 24.9 %copy-start.1 = (bf16[4,128,256]{2,1,0:T(8,128)(2,1)}, bf16[4,128,256]{2,1,0:T(8,128)(2,1)S(1)}, u32[]{:S(2)}) copy-start(bf16[4,128,256]{2,1,0:T(8,128)(2,1)S(1)} %constant_dynamic-update-slice_fusion.refs_3_.refs_1_) | copy-start | bytes 786436
  13.1 12.1 %collective-permute-start.7 = (bf16[4,128,256]{2,1,0:T(8,128)(2,1)S(1)}, bf16[4,128,256]{2,1,0:T(8,128)(2,1)S(1)}, u32[]{:S(2)}, u32[]{:S(2)}) collective-permute-start(bf16[4,128,256]{2,1,0:T(8,128)(2,1)S(1)} %constant_dynamic-update-slice_fusion.refs_3_.refs_1_), channel_id=1, source_target_pairs={{0,14},{1,15},{2,0},{3,1},{4,2},{5,3},{6,4},{7,5},{8,6},{9,7},{10,... | collective-permute-start | bytes 786440 | tf_op jit(solution)/shard_map/ppermute | solution.py:25
  16.6 12.3 %collective-permute-start.6 = (bf16[4,128,256]{2,1,0:T(8,128)(2,1)S(1)}, bf16[4,128,256]{2,1,0:T(8,128)(2,1)S(1)}, u32[]{:S(2)}, u32[]{:S(2)}) collective-permute-start(bf16[4,128,256]{2,1,0:T(8,128)(2,1)S(1)} %constant_dynamic-update-slice_fusion.refs_3_.refs_1_), channel_id=1, source_target_pairs={{0,2},{1,3},{2,4},{3,5},{4,6},{5,7},{6,8},{7,9},{8,10},{9,11},{10,... | collective-permute-start | bytes 786440 | tf_op jit(solution)/shard_map/ppermute | solution.py:25
  19.6 18.4 %copy-start.3 = (bf16[4,128,256]{2,1,0:T(8,128)(2,1)}, bf16[4,128,256]{2,1,0:T(8,128)(2,1)S(1)}, u32[]{:S(2)}) copy-start(bf16[4,128,256]{2,1,0:T(8,128)(2,1)S(1)} %collective-permute-done.5.refs_5_.refs_3_) | copy-start | bytes 786436
  19.6 11.2 %collective-permute-start.9 = (bf16[4,128,256]{2,1,0:T(8,128)(2,1)S(1)}, bf16[4,128,256]{2,1,0:T(8,128)(2,1)S(1)}, u32[]{:S(2)}, u32[]{:S(2)}) collective-permute-start(bf16[4,128,256]{2,1,0:T(8,128)(2,1)S(1)} %collective-permute-done.5.refs_5_.refs_3_), channel_id=1, source_target_pairs={{0,14},{1,15},{2,0},{3,1},{4,2},{5,3},{6,4},{7,5},{8,6},{9,7},{10,... | collective-permute-start | bytes 786440 | tf_op jit(solution)/shard_map/ppermute | solution.py:25
  23.3 14.7 %copy-start.4 = (bf16[4,128,256]{2,1,0:T(8,128)(2,1)}, bf16[4,128,256]{2,1,0:T(8,128)(2,1)S(1)}, u32[]{:S(2)}) copy-start(bf16[4,128,256]{2,1,0:T(8,128)(2,1)S(1)} %collective-permute-done.4.refs_4_.refs_2_) | copy-start | bytes 786436
  23.3 10.9 %collective-permute-start.8 = (bf16[4,128,256]{2,1,0:T(8,128)(2,1)S(1)}, bf16[4,128,256]{2,1,0:T(8,128)(2,1)S(1)}, u32[]{:S(2)}, u32[]{:S(2)}) collective-permute-start(bf16[4,128,256]{2,1,0:T(8,128)(2,1)S(1)} %collective-permute-done.4.refs_4_.refs_2_), channel_id=1, source_target_pairs={{0,2},{1,3},{2,4},{3,5},{4,6},{5,7},{6,8},{7,9},{8,10},{9,11},{10,... | collective-permute-start | bytes 786440 | tf_op jit(solution)/shard_map/ppermute | solution.py:25
  25.2 12.8 %copy-start.5 = (bf16[4,128,256]{2,1,0:T(8,128)(2,1)}, bf16[4,128,256]{2,1,0:T(8,128)(2,1)S(1)}, u32[]{:S(2)}) copy-start(bf16[4,128,256]{2,1,0:T(8,128)(2,1)S(1)} %collective-permute-done.7.refs_7_.refs_5_) | copy-start | bytes 786436
  25.2 9.4 %collective-permute-start.11 = (bf16[4,128,256]{2,1,0:T(8,128)(2,1)S(1)}, bf16[4,128,256]{2,1,0:T(8,128)(2,1)S(1)}, u32[]{:S(2)}, u32[]{:S(2)}) collective-permute-start(bf16[4,128,256]{2,1,0:T(8,128)(2,1)S(1)} %collective-permute-done.7.refs_7_.refs_5_), channel_id=1, source_target_pairs={{0,14},{1,15},{2,0},{3,1},{4,2},{5,3},{6,4},{7,5},{8,6},{9,7},{10,... | collective-permute-start | bytes 786440 | tf_op jit(solution)/shard_map/ppermute | solution.py:25
  28.9 9.2 %copy-start.6 = (bf16[4,128,256]{2,1,0:T(8,128)(2,1)}, bf16[4,128,256]{2,1,0:T(8,128)(2,1)S(1)}, u32[]{:S(2)}) copy-start(bf16[4,128,256]{2,1,0:T(8,128)(2,1)S(1)} %collective-permute-done.6.refs_6_.refs_4_) | copy-start | bytes 786436
  28.9 9.1 %collective-permute-start.10 = (bf16[4,128,256]{2,1,0:T(8,128)(2,1)S(1)}, bf16[4,128,256]{2,1,0:T(8,128)(2,1)S(1)}, u32[]{:S(2)}, u32[]{:S(2)}) collective-permute-start(bf16[4,128,256]{2,1,0:T(8,128)(2,1)S(1)} %collective-permute-done.6.refs_6_.refs_4_), channel_id=1, source_target_pairs={{0,2},{1,3},{2,4},{3,5},{4,6},{5,7},{6,8},{7,9},{8,10},{9,11},{10,... | collective-permute-start | bytes 786440 | tf_op jit(solution)/shard_map/ppermute | solution.py:25
  28.9 1.4 %collective-permute-start = (s32[1,64]{1,0:T(1,128)}, s32[1,64]{1,0:T(1,128)S(1)}, u32[]{:S(2)}, u32[]{:S(2)}) collective-permute-start(s32[1,64]{1,0:T(1,128)} %want_ref.1), channel_id=1, source_target_pairs={{0,1},{1,0},{2,3},{3,2},{4,5},{5,4},{6,7},{7,6},{8,9},{9,8},{10,11... | collective-permute-start | bytes 776 | tf_op jit(solution)/shard_map/ppermute | solution.py:25
  30.3 7.8 %copy-start.20 = (s32[1,64]{1,0:T(1,128)}, s32[1,64]{1,0:T(1,128)S(1)}, u32[]{:S(2)}) copy-start(s32[1,64]{1,0:T(1,128)S(1)} %collective-permute-done.refs_0_) | copy-start | bytes 772
  30.8 7.2 %copy-start.7 = (bf16[4,128,256]{2,1,0:T(8,128)(2,1)}, bf16[4,128,256]{2,1,0:T(8,128)(2,1)S(1)}, u32[]{:S(2)}) copy-start(bf16[4,128,256]{2,1,0:T(8,128)(2,1)S(1)} %collective-permute-done.9.refs_9_.refs_7_) | copy-start | bytes 786436
  34.2 3.8 %copy-start.8 = (bf16[4,128,256]{2,1,0:T(8,128)(2,1)}, bf16[4,128,256]{2,1,0:T(8,128)(2,1)S(1)}, u32[]{:S(2)}) copy-start(bf16[4,128,256]{2,1,0:T(8,128)(2,1)S(1)} %collective-permute-done.8.refs_8_.refs_6_) | copy-start | bytes 786436
  34.6 3.5 %copy-start.9 = (bf16[4,128,256]{2,1,0:T(8,128)(2,1)}, bf16[4,128,256]{2,1,0:T(8,128)(2,1)S(1)}, u32[]{:S(2)}) copy-start(bf16[4,128,256]{2,1,0:T(8,128)(2,1)S(1)} %collective-permute-done.11.refs_11_.refs_9_) | copy-start | bytes 786436
  38.1 0.8 copy-start.10
  41.8 22.0 %copy-start.21 = (s32[24,2]{0,1:T(2,128)S(1)}, s32[24,2]{0,1:T(2,128)}, u32[]{:S(2)}) copy-start(s32[24,2]{0,1:T(2,128)} %param.12) | copy-start | bytes 580
  41.9 23.4 %collective-permute-start.12 = (bf16[20,128,256]{2,1,0:T(8,128)(2,1)}, bf16[20,128,256]{2,1,0:T(8,128)(2,1)S(1)}, u32[]{:S(2)}, u32[]{:S(2)}) collective-permute-start(bf16[20,128,256]{2,1,0:T(8,128)(2,1)} %pick.2), channel_id=1, source_target_pairs={{0,1},{1,0},{2,3},{3,2},{4,5},{5,4},{6,7},{7,6},{8,9},{9,8},{10,11... | collective-permute-start | bytes 3932168 | tf_op jit(solution)/shard_map/ppermute | solution.py:25
  42.0 10.7 %collective-permute-start.13 = (bf16[4,128,256]{2,1,0:T(8,128)(2,1)}, bf16[4,128,256]{2,1,0:T(8,128)(2,1)S(1)}, u32[]{:S(2)}, u32[]{:S(2)}) collective-permute-start(bf16[4,128,256]{2,1,0:T(8,128)(2,1)} %copy-done.8), channel_id=1, source_target_pairs={{0,2},{1,3},{2,4},{3,5},{4,6},{5,7},{6,8},{7,9},{8,10},{9,11},{10,... | collective-permute-start | bytes 786440 | tf_op jit(solution)/shard_map/ppermute | solution.py:25
  42.0 10.6 %collective-permute-start.16 = (bf16[4,128,256]{2,1,0:T(8,128)(2,1)}, bf16[4,128,256]{2,1,0:T(8,128)(2,1)S(1)}, u32[]{:S(2)}, u32[]{:S(2)}) collective-permute-start(bf16[4,128,256]{2,1,0:T(8,128)(2,1)} %copy-done.9), channel_id=1, source_target_pairs={{0,14},{1,15},{2,0},{3,1},{4,2},{5,3},{6,4},{7,5},{8,6},{9,7},{10,... | collective-permute-start | bytes 786440 | tf_op jit(solution)/shard_map/ppermute | solution.py:25
  45.3 12.6 %collective-permute-start.14 = (bf16[4,128,256]{2,1,0:T(8,128)(2,1)}, bf16[4,128,256]{2,1,0:T(8,128)(2,1)S(1)}, u32[]{:S(2)}, u32[]{:S(2)}) collective-permute-start(bf16[4,128,256]{2,1,0:T(8,128)(2,1)} %copy-done.7), channel_id=1, source_target_pairs={{0,14},{1,15},{2,0},{3,1},{4,2},{5,3},{6,4},{7,5},{8,6},{9,7},{10,... | collective-permute-start | bytes 786440 | tf_op jit(solution)/shard_map/ppermute | solution.py:25
  45.3 13.0 %collective-permute-start.15 = (bf16[4,128,256]{2,1,0:T(8,128)(2,1)}, bf16[4,128,256]{2,1,0:T(8,128)(2,1)S(1)}, u32[]{:S(2)}, u32[]{:S(2)}) collective-permute-start(bf16[4,128,256]{2,1,0:T(8,128)(2,1)} %copy-done.10), channel_id=1, source_target_pairs={{0,2},{1,3},{2,4},{3,5},{4,6},{5,7},{6,8},{7,9},{8,10},{9,11},{10,... | collective-permute-start | bytes 786440 | tf_op jit(solution)/shard_map/ppermute | solution.py:25
  52.6 5.6 %copy-start.11 = (bf16[4,128,256]{2,1,0:T(8,128)(2,1)}, bf16[4,128,256]{2,1,0:T(8,128)(2,1)S(1)}, u32[]{:S(2)}) copy-start(bf16[4,128,256]{2,1,0:T(8,128)(2,1)S(1)} %collective-permute-done.13.refs_2_.refs_10_) | copy-start | bytes 786436
  52.6 10.7 %collective-permute-start.18 = (bf16[4,128,256]{2,1,0:T(8,128)(2,1)S(1)}, bf16[4,128,256]{2,1,0:T(8,128)(2,1)S(1)}, u32[]{:S(2)}, u32[]{:S(2)}) collective-permute-start(bf16[4,128,256]{2,1,0:T(8,128)(2,1)S(1)} %collective-permute-done.13.refs_2_.refs_10_), channel_id=1, source_target_pairs={{0,2},{1,3},{2,4},{3,5},{4,6},{5,7},{6,8},{7,9},{8,10},{9,11},{10,... | collective-permute-start | bytes 786440 | tf_op jit(solution)/shard_map/ppermute | solution.py:25
  52.6 5.6 %copy-start.12 = (bf16[4,128,256]{2,1,0:T(8,128)(2,1)}, bf16[4,128,256]{2,1,0:T(8,128)(2,1)S(1)}, u32[]{:S(2)}) copy-start(bf16[4,128,256]{2,1,0:T(8,128)(2,1)S(1)} %collective-permute-done.16.refs_5_.refs_13_) | copy-start | bytes 786436
  52.7 10.7 %collective-permute-start.20 = (bf16[4,128,256]{2,1,0:T(8,128)(2,1)S(1)}, bf16[4,128,256]{2,1,0:T(8,128)(2,1)S(1)}, u32[]{:S(2)}, u32[]{:S(2)}) collective-permute-start(bf16[4,128,256]{2,1,0:T(8,128)(2,1)S(1)} %collective-permute-done.16.refs_5_.refs_13_), channel_id=1, source_target_pairs={{0,14},{1,15},{2,0},{3,1},{4,2},{5,3},{6,4},{7,5},{8,6},{9,7},{10,... | collective-permute-start | bytes 786440 | tf_op jit(solution)/shard_map/ppermute | solution.py:25
  57.9 0.7 copy-start.13
  58.6 0.7 copy-start.14
  61.9 3.4 %collective-permute-start.17 = (bf16[8,128,256]{2,1,0:T(8,128)(2,1)}, bf16[8,128,256]{2,1,0:T(8,128)(2,1)S(1)}, u32[]{:S(2)}, u32[]{:S(2)}) collective-permute-start(bf16[8,128,256]{2,1,0:T(8,128)(2,1)} %pick.3), channel_id=1, source_target_pairs={{0,1},{1,0},{2,3},{3,2},{4,5},{5,4},{6,7},{7,6},{8,9},{9,8},{10,11... | collective-permute-start | bytes 1572872 | tf_op jit(solution)/shard_map/ppermute | solution.py:25
  63.3 1.9 %copy-start.16 = (bf16[4,128,256]{2,1,0:T(8,128)(2,1)}, bf16[4,128,256]{2,1,0:T(8,128)(2,1)S(1)}, u32[]{:S(2)}) copy-start(bf16[4,128,256]{2,1,0:T(8,128)(2,1)S(1)} %collective-permute-done.18.refs_14_) | copy-start | bytes 786436
  63.3 1.5 %collective-permute-start.19 = (bf16[4,128,256]{2,1,0:T(8,128)(2,1)S(1)}, bf16[4,128,256]{2,1,0:T(8,128)(2,1)S(1)}, u32[]{:S(2)}, u32[]{:S(2)}) collective-permute-start(bf16[4,128,256]{2,1,0:T(8,128)(2,1)S(1)} %collective-permute-done.18.refs_14_), channel_id=1, source_target_pairs={{0,1},{1,0},{2,3},{3,2},{4,5},{5,4},{6,7},{7,6},{8,9},{9,8},{10,11... | collective-permute-start | bytes 786440 | tf_op jit(solution)/shard_map/ppermute | solution.py:25
  63.3 1.9 %copy-start.17 = (bf16[4,128,256]{2,1,0:T(8,128)(2,1)}, bf16[4,128,256]{2,1,0:T(8,128)(2,1)S(1)}, u32[]{:S(2)}) copy-start(bf16[4,128,256]{2,1,0:T(8,128)(2,1)S(1)} %collective-permute-done.20.refs_15_) | copy-start | bytes 786436
  63.3 1.9 %collective-permute-start.21 = (bf16[4,128,256]{2,1,0:T(8,128)(2,1)S(1)}, bf16[4,128,256]{2,1,0:T(8,128)(2,1)S(1)}, u32[]{:S(2)}, u32[]{:S(2)}) collective-permute-start(bf16[4,128,256]{2,1,0:T(8,128)(2,1)S(1)} %collective-permute-done.20.refs_15_), channel_id=1, source_target_pairs={{0,1},{1,0},{2,3},{3,2},{4,5},{5,4},{6,7},{7,6},{8,9},{9,8},{10,11... | collective-permute-start | bytes 786440 | tf_op jit(solution)/shard_map/ppermute | solution.py:25
  64.9 0.7 copy-start.18
  65.2 0.7 copy-start.19
  65.2 0.9 copy-start.15
  66.1 1.1 copy-start.2
  80.0 2.6 %collective-permute-start.22 = (f32[32,8,768]{2,1,0:T(8,128)}, f32[32,8,768]{2,1,0:T(8,128)S(1)}, u32[]{:S(2)}, u32[]{:S(2)}) collective-permute-start(f32[32,8,768]{2,1,0:T(8,128)} %get-tuple-element.16), channel_id=1, source_target_pairs={{0,1},{1,0},{2,3},{3,2},{4,5},{5,4},{6,7},{7,6},{8,9},{9,8},{10,11... | collective-permute-start | bytes 2359304 | tf_op jit(solution)/shard_map/ppermute | solution.py:25
  83.8 5.8 %collective-permute-start.23 = (bf16[8,8,768]{2,1,0:T(8,128)(2,1)S(1)}, bf16[8,8,768]{2,1,0:T(8,128)(2,1)S(1)}, u32[]{:S(2)}, u32[]{:S(2)}) collective-permute-start(bf16[8,8,768]{2,1,0:T(8,128)(2,1)S(1)} %get-tuple-element.19), channel_id=1, source_target_pairs={{0,16},{1,17},{2,18},{3,19},{4,20},{5,21},{6,22},{7,23},{8,24},{9,... | collective-permute-start | bytes 294920 | tf_op jit(solution)/shard_map/ppermute | solution.py:25
  85.3 7.2 %collective-permute-start.25 = (bf16[8,8,768]{2,1,0:T(8,128)(2,1)S(1)}, bf16[8,8,768]{2,1,0:T(8,128)(2,1)S(1)}, u32[]{:S(2)}, u32[]{:S(2)}) collective-permute-start(bf16[8,8,768]{2,1,0:T(8,128)(2,1)S(1)} %get-tuple-element.20), channel_id=1, source_target_pairs={{0,32},{1,33},{2,34},{3,35},{4,36},{5,37},{6,38},{7,39},{8,40},{9,... | collective-permute-start | bytes 294920 | tf_op jit(solution)/shard_map/ppermute | solution.py:25
  87.5 6.2 %collective-permute-start.24 = (bf16[8,8,768]{2,1,0:T(8,128)(2,1)S(1)}, bf16[8,8,768]{2,1,0:T(8,128)(2,1)S(1)}, u32[]{:S(2)}, u32[]{:S(2)}) collective-permute-start(bf16[8,8,768]{2,1,0:T(8,128)(2,1)S(1)} %get-tuple-element.21), channel_id=1, source_target_pairs={{0,48},{1,49},{2,50},{3,51},{4,52},{5,53},{6,54},{7,55},{8,56},{9,... | collective-permute-start | bytes 294920 | tf_op jit(solution)/shard_map/ppermute | solution.py:25
  106.7 17.2 %collective-permute-start.28 = (f32[8,768]{1,0:T(8,128)S(1)}, f32[8,768]{1,0:T(8,128)S(1)}, u32[]{:S(2)}, u32[]{:S(2)}) collective-permute-start(f32[8,768]{1,0:T(8,128)S(1)} %convert_reduce_fusion), channel_id=1, source_target_pairs={{0,192},{64,128},{128,64},{192,0},{1,193},{65,129},{129,65},{193,1... | collective-permute-start | bytes 73736 | tf_op jit(solution)/shard_map/ppermute | solution.py:377
  109.7 14.2 %collective-permute-start.27 = (f32[8,768]{1,0:T(8,128)S(1)}, f32[8,768]{1,0:T(8,128)S(1)}, u32[]{:S(2)}, u32[]{:S(2)}) collective-permute-start(f32[8,768]{1,0:T(8,128)S(1)} %convert_reduce_fusion), channel_id=1, source_target_pairs={{0,128},{64,192},{128,0},{192,64},{1,129},{65,193},{129,1},{193,65... | collective-permute-start | bytes 73736 | tf_op jit(solution)/shard_map/ppermute | solution.py:377
  110.5 13.5 %collective-permute-start.26 = (f32[8,768]{1,0:T(8,128)S(1)}, f32[8,768]{1,0:T(8,128)S(1)}, u32[]{:S(2)}, u32[]{:S(2)}) collective-permute-start(f32[8,768]{1,0:T(8,128)S(1)} %convert_reduce_fusion), channel_id=1, source_target_pairs={{0,64},{64,0},{128,192},{192,128},{1,65},{65,1},{129,193},{193,129... | collective-permute-start | bytes 73736 | tf_op jit(solution)/shard_map/ppermute | solution.py:377

commit v2 on v1

--- a/solution.py
+++ b/solution.py
@@ -284,7 +284,7 @@
     )(neighbor, counts, wanted, position, features, *blocks, adjacency, features, cotangent, weight_in, weight_out)
 
 
-def join_gradient(grad_preact, weight_in, half, before=()):
+def join_gradient(grad_preact, weight_in, begin, end, before=()):
     nodes, hid = grad_preact.shape
     channels = weight_in.shape[0] // 2
     tile = nodes // 4
@@ -297,14 +297,14 @@
 
     return pl.pallas_call(
         kernel,
-        grid=(2,),
+        grid=(end - begin,),
         out_shape=[jax.ShapeDtypeStruct((nodes, channels), t) for t in (BF, F32)],
         in_specs=[
-            pl.BlockSpec((tile, hid), lambda i: (i + 2 * half, 0)),
+            pl.BlockSpec((tile, hid), lambda i: (i + begin, 0)),
             pl.BlockSpec(weight_in.shape, lambda i: (0, 0), pipeline_mode=pl.Buffered(1)),
         ]
         + [pl.BlockSpec(memory_space=pl.ANY)] * len(before),
-        out_specs=[pl.BlockSpec((tile, channels), lambda i: (i + 2 * half, 0))] * 2,
+        out_specs=[pl.BlockSpec((tile, channels), lambda i: (i + begin, 0))] * 2,
         input_output_aliases={2 + i: i for i in range(len(before))},
         name="joingrad",
     )(grad_preact, weight_in, *before)
@@ -401,8 +401,8 @@
         features, (given, given_third, *far[2:], *near.arrays, *far[:2]), adjacency, cotangent, weight_in, weight_out,
         neighbor, counts, wanted, position, scale,
     )
-    joined = join_gradient(grad_preact, weight_in, 0)
-    grad_aggregate, right = join_gradient(grad_preact, weight_in, 1, joined)
+    joined = join_gradient(grad_preact, weight_in, 0, 1)
+    grad_aggregate, right = join_gradient(grad_preact, weight_in, 1, 4, joined)
     grad_features = scatter_gradient(grad_aggregate, right, adjacency, neighbor, counts)
     total = reduce_terms(keep, send, hid)
     return (grad_features, *total)

time: 127 us -> 128 us (level)
  transfers between devices with their start and end apart: 29 -> 29, of which waited for: 16 -> 16; matrix products, arithmetic and copies ran while one was open for 1% -> 1% of each run, Pallas kernels for 12% -> 13%
where the time goes in v2:
time: 128 us; the launch traced here: 126 us
  starting transfers between devices  41.7 us (33%)
  Pallas kernels  32.4 us (25%)
  waiting for transfers between devices  29.5 us (23%)
  blocking collectives  12.9 us (10%)
  local copies, waits for them, and re-layouts  4.57 us (4%)
  other arithmetic  4.17 us (3%)
    ppermute x26, starting transfers between devices, move(): return lax.ppermute(a, 'dom', pairs)  37.6 us
    ppermute x26, waiting for transfers between devices, move(): return lax.ppermute(a, 'dom', pairs)  29.5 us
    all_to_all x1, blocking collectives, reduce_terms(): lax.all_to_all(keep, 'dom', 0, 0, axis_index_groups=columns).astype(F32)  12.9 us
    pallas_call x1, Pallas kernels, forward(): pl.pallas_call(kernel, grid=(steps,), out_shape=[jax.ShapeDtypeStruct((no...  12.8 us
    pallas_call x2, Pallas kernels, join_gradient(): pl.pallas_call(kernel, grid=(end - begin,), out_shape=[jax.ShapeDtypeStru...  8.11 us
    pallas_call x1, Pallas kernels, scatter_gradient(): pl.pallas_call(kernel, grid=(steps,), out_shape=jax.ShapeDtypeStruct((nod...  5.96 us
    pallas_call x2, Pallas kernels, pick(): pl.pallas_call(kernel, out_shape=[jax.ShapeDtypeStruct((count, *block), B...  5.5 us
    unnamed x46, local copies, waits for them, and re-layouts  4.54 us
  transfers between devices with their start and end apart: 29, of which 16 were waited for; matrix products, arithmetic and copies ran while one was open for 1% of the time, Pallas kernels for 13%

profile of v2, /device:TPU:2, one launch (start us, length us, event | category | flops | bytes accessed | tf_op | source)
XLA Modules:
  0.0 126.2 jit_solution(2583319223701499738)
XLA Ops:
  0.6 1.0 convert_element_type.20
  1.6 2.3 %collective-permute-start.1 = (bf16[2,128,256]{2,1,0:T(8,128)(2,1)S(1)}, bf16[2,128,256]{2,1,0:T(8,128)(2,1)S(1)}, u32[]{:S(2)}, u32[]{:S(2)}) collective-permute-start(bf16[2,128,256]{2,1,0:T(8,128)(2,1)S(1)} %bitcast.4), channel_id=1, source_target_pairs={{0,48},{1,49},{2,50},{3,51},{4,52},{5,53},{6,54},{7,55},{8,56},{9,... | collective-permute-start | bytes 393224 | tf_op jit(solution)/shard_map/ppermute | solution.py:25
  3.9 3.1 %collective-permute-start.3 = (bf16[2,128,256]{2,1,0:T(8,128)(2,1)S(1)}, bf16[2,128,256]{2,1,0:T(8,128)(2,1)S(1)}, u32[]{:S(2)}, u32[]{:S(2)}) collective-permute-start(bf16[2,128,256]{2,1,0:T(8,128)(2,1)S(1)} %bitcast.6), channel_id=1, source_target_pairs={{0,32},{1,33},{2,34},{3,35},{4,36},{5,37},{6,38},{7,39},{8,40},{9,... | collective-permute-start | bytes 393224 | tf_op jit(solution)/shard_map/ppermute | solution.py:25
  7.1 5.9 %collective-permute-start.5 = (bf16[4,128,256]{2,1,0:T(8,128)(2,1)S(1)}, bf16[4,128,256]{2,1,0:T(8,128)(2,1)S(1)}, u32[]{:S(2)}, u32[]{:S(2)}) collective-permute-start(bf16[4,128,256]{2,1,0:T(8,128)(2,1)S(1)} %pad_maximum_fusion.refs_2_.refs_0_), channel_id=1, source_target_pairs={{0,14},{1,15},{2,0},{3,1},{4,2},{5,3},{6,4},{7,5},{8,6},{9,7},{10,... | collective-permute-start | bytes 786440 | tf_op jit(solution)/shard_map/ppermute | solution.py:25
  13.0 0.0 collective-permute-done.3
  13.1 3.5 %collective-permute-start.7 = (bf16[4,128,256]{2,1,0:T(8,128)(2,1)S(1)}, bf16[4,128,256]{2,1,0:T(8,128)(2,1)S(1)}, u32[]{:S(2)}, u32[]{:S(2)}) collective-permute-start(bf16[4,128,256]{2,1,0:T(8,128)(2,1)S(1)} %constant_dynamic-update-slice_fusion.refs_3_.refs_1_), channel_id=1, source_target_pairs={{0,14},{1,15},{2,0},{3,1},{4,2},{5,3},{6,4},{7,5},{8,6},{9,7},{10,... | collective-permute-start | bytes 786440 | tf_op jit(solution)/shard_map/ppermute | solution.py:25
  16.6 0.0 collective-permute-start.6
  16.6 3.0 %collective-permute-done.5.refs_5_.refs_3_ = bf16[4,128,256]{2,1,0:T(8,128)(2,1)S(1)} collective-permute-done((bf16[4,128,256]{2,1,0:T(8,128)(2,1)S(1)}, bf16[4,128,256]{2,1,0:T(8,128)(2,1)S(1)}, u32[]{:S(2)}, u32[]{:S(2)}) %collective-permute-start.5) | collective-permute-done | bytes 262176 | tf_op jit(solution)/shard_map/ppermute | solution.py:25
  19.6 3.7 %collective-permute-start.9 = (bf16[4,128,256]{2,1,0:T(8,128)(2,1)S(1)}, bf16[4,128,256]{2,1,0:T(8,128)(2,1)S(1)}, u32[]{:S(2)}, u32[]{:S(2)}) collective-permute-start(bf16[4,128,256]{2,1,0:T(8,128)(2,1)S(1)} %collective-permute-done.5.refs_5_.refs_3_), channel_id=1, source_target_pairs={{0,14},{1,15},{2,0},{3,1},{4,2},{5,3},{6,4},{7,5},{8,6},{9,7},{10,... | collective-permute-start | bytes 786440 | tf_op jit(solution)/shard_map/ppermute | solution.py:25
  23.3 1.9 %collective-permute-done.7.refs_7_.refs_5_ = bf16[4,128,256]{2,1,0:T(8,128)(2,1)S(1)} collective-permute-done((bf16[4,128,256]{2,1,0:T(8,128)(2,1)S(1)}, bf16[4,128,256]{2,1,0:T(8,128)(2,1)S(1)}, u32[]{:S(2)}, u32[]{:S(2)}) %collective-permute-start.7) | collective-permute-done | bytes 262176 | tf_op jit(solution)/shard_map/ppermute | solution.py:25
  25.2 3.7 %collective-permute-start.11 = (bf16[4,128,256]{2,1,0:T(8,128)(2,1)S(1)}, bf16[4,128,256]{2,1,0:T(8,128)(2,1)S(1)}, u32[]{:S(2)}, u32[]{:S(2)}) collective-permute-start(bf16[4,128,256]{2,1,0:T(8,128)(2,1)S(1)} %collective-permute-done.7.refs_7_.refs_5_), channel_id=1, source_target_pairs={{0,14},{1,15},{2,0},{3,1},{4,2},{5,3},{6,4},{7,5},{8,6},{9,7},{10,... | collective-permute-start | bytes 786440 | tf_op jit(solution)/shard_map/ppermute | solution.py:25
  28.9 0.0 collective-permute-done.6.refs_6_.refs_4_
  28.9 0.0 collective-permute-start.10
  28.9 0.1 collective-permute-start
  29.0 0.7 pad_add_fusion.refs_1_.at_ref
  29.7 0.6 collective-permute-done.refs_0_
  30.3 0.5 collective-permute-done.9.refs_9_.refs_7_
  30.8 3.4 %collective-permute-done.8.refs_8_.refs_6_ = bf16[4,128,256]{2,1,0:T(8,128)(2,1)S(1)} collective-permute-done((bf16[4,128,256]{2,1,0:T(8,128)(2,1)S(1)}, bf16[4,128,256]{2,1,0:T(8,128)(2,1)S(1)}, u32[]{:S(2)}, u32[]{:S(2)}) %collective-permute-start.8) | collective-permute-done | bytes 262176 | tf_op jit(solution)/shard_map/ppermute | solution.py:25
  34.2 0.4 collective-permute-done.11.refs_11_.refs_9_
  34.6 3.4 %collective-permute-done.10.refs_10_.refs_8_ = bf16[4,128,256]{2,1,0:T(8,128)(2,1)S(1)} collective-permute-done((bf16[4,128,256]{2,1,0:T(8,128)(2,1)S(1)}, bf16[4,128,256]{2,1,0:T(8,128)(2,1)S(1)}, u32[]{:S(2)}, u32[]{:S(2)}) %collective-permute-start.10) | collective-permute-done | bytes 262176 | tf_op jit(solution)/shard_map/ppermute | solution.py:25
  38.1 0.7 copy-done.10
  38.8 3.0 %pick.2 = bf16[20,128,256]{2,1,0:T(8,128)(2,1)} custom-call(s32[1,64]{1,0:T(1,128)} %copy-done.20, s32[3]{0:T(128)} %pad_add_fusion.refs_1_.at_ref, bf16[4,128,256]{2,1,0:T(8,128)(2,1)} %copy-done, bf16[4,128,256]{2,1,0:T(8,128)(2,1)} %copy-done.1, bf16[4,128,256]{2,1,0:T(8,128)(2,1)} %copy-done.4, bf16[4,128,256]{2,1,0:T(8,128)(2,1)} %copy-done.3, ...), custom_call_target="tpu_custom_call" | custom-call | tf_op jit(solution)/shard_map/pick/pallas_call | solution.py:98
  41.8 0.0 copy-start.21
  41.9 0.1 collective-permute-start.12
  42.0 0.1 collective-permute-start.13
  42.0 3.2 %collective-permute-start.16 = (bf16[4,128,256]{2,1,0:T(8,128)(2,1)}, bf16[4,128,256]{2,1,0:T(8,128)(2,1)S(1)}, u32[]{:S(2)}, u32[]{:S(2)}) collective-permute-start(bf16[4,128,256]{2,1,0:T(8,128)(2,1)} %copy-done.9), channel_id=1, source_target_pairs={{0,14},{1,15},{2,0},{3,1},{4,2},{5,3},{6,4},{7,5},{8,6},{9,7},{10,... | collective-permute-start | bytes 786440 | tf_op jit(solution)/shard_map/ppermute | solution.py:25
  45.3 0.0 collective-permute-start.14
  45.3 2.0 %collective-permute-start.15 = (bf16[4,128,256]{2,1,0:T(8,128)(2,1)}, bf16[4,128,256]{2,1,0:T(8,128)(2,1)S(1)}, u32[]{:S(2)}, u32[]{:S(2)}) collective-permute-start(bf16[4,128,256]{2,1,0:T(8,128)(2,1)} %copy-done.10), channel_id=1, source_target_pairs={{0,2},{1,3},{2,4},{3,5},{4,6},{5,7},{6,8},{7,9},{8,10},{9,11},{10,... | collective-permute-start | bytes 786440 | tf_op jit(solution)/shard_map/ppermute | solution.py:25
  47.3 5.3 %collective-permute-done.13.refs_2_.refs_10_ = bf16[4,128,256]{2,1,0:T(8,128)(2,1)S(1)} collective-permute-done((bf16[4,128,256]{2,1,0:T(8,128)(2,1)}, bf16[4,128,256]{2,1,0:T(8,128)(2,1)S(1)}, u32[]{:S(2)}, u32[]{:S(2)}) %collective-permute-start.13) | collective-permute-done | bytes 262176 | tf_op jit(solution)/shard_map/ppermute | solution.py:25
  52.7 3.2 %collective-permute-start.20 = (bf16[4,128,256]{2,1,0:T(8,128)(2,1)S(1)}, bf16[4,128,256]{2,1,0:T(8,128)(2,1)S(1)}, u32[]{:S(2)}, u32[]{:S(2)}) collective-permute-start(bf16[4,128,256]{2,1,0:T(8,128)(2,1)S(1)} %collective-permute-done.16.refs_5_.refs_13_), channel_id=1, source_target_pairs={{0,14},{1,15},{2,0},{3,1},{4,2},{5,3},{6,4},{7,5},{8,6},{9,7},{10,... | collective-permute-start | bytes 786440 | tf_op jit(solution)/shard_map/ppermute | solution.py:25
  55.9 2.0 %collective-permute-done.14.refs_3_.refs_11_ = bf16[4,128,256]{2,1,0:T(8,128)(2,1)S(1)} collective-permute-done((bf16[4,128,256]{2,1,0:T(8,128)(2,1)}, bf16[4,128,256]{2,1,0:T(8,128)(2,1)S(1)}, u32[]{:S(2)}, u32[]{:S(2)}) %collective-permute-start.14) | collective-permute-done | bytes 262176 | tf_op jit(solution)/shard_map/ppermute | solution.py:25
  57.9 0.3 collective-permute-done.15.refs_4_.refs_12_
  58.3 0.4 copy-done.13
  58.6 0.7 copy-done.14
  59.4 2.5 %pick.3 = bf16[8,128,256]{2,1,0:T(8,128)(2,1)} custom-call(s32[1,64]{1,0:T(1,128)} %copy-done.20, s32[3]{0:T(128)} %pad_add_fusion.refs_1_.at_ref, bf16[4,128,256]{2,1,0:T(8,128)(2,1)} %copy-done.11, bf16[4,128,256]{2,1,0:T(8,128)(2,1)} %copy-done.13, bf16[4,128,256]{2,1,0:T(8,128)(2,1)} %copy-done.14, bf16[4,128,256]{2,1,0:T(8,128)(2,1)} %copy-done.12), custom_call_target="tpu_custom_call" | custom-call | tf_op jit(solution)/shard_map/pick/pallas_call | solution.py:98
  61.9 0.1 collective-permute-start.17
  62.0 1.4 %collective-permute-done.18.refs_14_ = bf16[4,128,256]{2,1,0:T(8,128)(2,1)S(1)} collective-permute-done((bf16[4,128,256]{2,1,0:T(8,128)(2,1)S(1)}, bf16[4,128,256]{2,1,0:T(8,128)(2,1)S(1)}, u32[]{:S(2)}, u32[]{:S(2)}) %collective-permute-start.18) | collective-permute-done | bytes 262176 | tf_op jit(solution)/shard_map/ppermute | solution.py:25
  63.3 0.5 collective-permute-start.21
  63.8 0.7 copy.15.nb_ref
  64.5 0.3 collective-permute-done.19.given_p
  64.9 0.4 collective-permute-done.21.given_q
  65.3 0.3 copy-done.18
  65.6 0.4 copy-done.19
  65.9 0.2 copy-done.15
  66.2 1.1 copy-done.2
  67.2 12.8 %forward.1 = (bf16[3072,512]{1,0:T(8,128)(2,1)}, f32[32,8,768]{2,1,0:T(8,128)}, f32[32,8,768]{2,1,0:T(8,128)}) custom-call(s32[24,2]{1,0:T(8,128)} %copy.15.nb_ref, s32[24]{0:T(128)} %cnt_ref.3, s32[1,64]{1,0:T(1,128)} %want_ref.1, s32[3]{0:T(128)} %pad_add_fusion.refs_1_.at_ref, bf16[3072,256]{1,0:T(8,128)(2,1)} %refs_17_.1, ...), custom_call_target="tpu_custom_call" | custom-call | tf_op jit(solution)/shard_map/forward/pallas_call | solution.py:260
  80.0 0.1 collective-permute-start.22
  80.1 2.5 %collective-permute-done.22 = f32[32,8,768]{2,1,0:T(8,128)S(1)} collective-permute-done((f32[32,8,768]{2,1,0:T(8,128)}, f32[32,8,768]{2,1,0:T(8,128)S(1)}, u32[]{:S(2)}, u32[]{:S(2)}) %collective-permute-start.22) | collective-permute-done | bytes 786464 | tf_op jit(solution)/shard_map/ppermute | solution.py:25
  82.6 1.2 fusion.5
  83.8 1.5 %collective-permute-start.23 = (bf16[8,8,768]{2,1,0:T(8,128)(2,1)S(1)}, bf16[8,8,768]{2,1,0:T(8,128)(2,1)S(1)}, u32[]{:S(2)}, u32[]{:S(2)}) collective-permute-start(bf16[8,8,768]{2,1,0:T(8,128)(2,1)S(1)} %get-tuple-element.19), channel_id=1, source_target_pairs={{0,16},{1,17},{2,18},{3,19},{4,20},{5,21},{6,22},{7,23},{8,24},{9,... | collective-permute-start | bytes 294920 | tf_op jit(solution)/shard_map/ppermute | solution.py:25
  85.3 2.2 %collective-permute-start.25 = (bf16[8,8,768]{2,1,0:T(8,128)(2,1)S(1)}, bf16[8,8,768]{2,1,0:T(8,128)(2,1)S(1)}, u32[]{:S(2)}, u32[]{:S(2)}) collective-permute-start(bf16[8,8,768]{2,1,0:T(8,128)(2,1)S(1)} %get-tuple-element.20), channel_id=1, source_target_pairs={{0,32},{1,33},{2,34},{3,35},{4,36},{5,37},{6,38},{7,39},{8,40},{9,... | collective-permute-start | bytes 294920 | tf_op jit(solution)/shard_map/ppermute | solution.py:25
  87.5 2.2 %collective-permute-start.24 = (bf16[8,8,768]{2,1,0:T(8,128)(2,1)S(1)}, bf16[8,8,768]{2,1,0:T(8,128)(2,1)S(1)}, u32[]{:S(2)}, u32[]{:S(2)}) collective-permute-start(bf16[8,8,768]{2,1,0:T(8,128)(2,1)S(1)} %get-tuple-element.21), channel_id=1, source_target_pairs={{0,48},{1,49},{2,50},{3,51},{4,52},{5,53},{6,54},{7,55},{8,56},{9,... | collective-permute-start | bytes 294920 | tf_op jit(solution)/shard_map/ppermute | solution.py:25
  89.7 2.8 %collective-permute-done.25 = bf16[8,8,768]{2,1,0:T(8,128)(2,1)S(1)} collective-permute-done((bf16[8,8,768]{2,1,0:T(8,128)(2,1)S(1)}, bf16[8,8,768]{2,1,0:T(8,128)(2,1)S(1)}, u32[]{:S(2)}, u32[]{:S(2)}) %collective-permute-start.25) | collective-permute-done | bytes 98336 | tf_op jit(solution)/shard_map/ppermute | solution.py:25
  92.5 1.2 collective-permute-done.24
  93.7 0.1 fusion.2
  93.8 12.9 %all_to_all.5 = bf16[8,8,768]{2,1,0:T(8,128)(2,1)S(1)} all-to-all(bf16[8,8,768]{2,1,0:T(8,128)(2,1)S(1)} %fusion.2), channel_id=1, replica_groups={{0,2,4,6,8,10,12,14},{1,3,5,7,9,11,13,15},{16,18,20,22,24,26,28,30},{17..., dimensions={0} | all-to-all | bytes 196608 | tf_op jit(solution)/shard_map/all_to_all | solution.py:374
  106.7 3.0 %collective-permute-start.28 = (f32[8,768]{1,0:T(8,128)S(1)}, f32[8,768]{1,0:T(8,128)S(1)}, u32[]{:S(2)}, u32[]{:S(2)}) collective-permute-start(f32[8,768]{1,0:T(8,128)S(1)} %convert_reduce_fusion), channel_id=1, source_target_pairs={{0,192},{64,128},{128,64},{192,0},{1,193},{65,129},{129,65},{193,1... | collective-permute-start | bytes 73736 | tf_op jit(solution)/shard_map/ppermute | solution.py:377
  109.7 0.7 collective-permute-start.27
  110.5 0.4 collective-permute-start.26
  110.9 2.9 %joingrad.2 = (bf16[3072,256]{1,0:T(8,128)(2,1)}, f32[3072,256]{1,0:T(8,128)}) custom-call(bf16[3072,512]{1,0:T(8,128)(2,1)} %get-tuple-element.10.gp, bf16[512,512]{1,0:T(8,128)(2,1)} %win.3), custom_call_target="tpu_custom_call" | custom-call | tf_op jit(solution)/shard_map/joingrad/pallas_call | solution.py:298
  113.8 5.2 %joingrad.3 = (bf16[3072,256]{1,0:T(8,128)(2,1)}, f32[3072,256]{1,0:T(8,128)}) custom-call(bf16[3072,512]{1,0:T(8,128)(2,1)} %get-tuple-element.10.gp, bf16[512,512]{1,0:T(8,128)(2,1)} %win.3, bf16[3072,256]{1,0:T(8,128)(2,1)} %get-tuple-element.11.refs_0_, f32[3072,256]{1,0:T(8,128)} %get-tuple-element.12.refs_1_), custom_call_target="tpu_custom_call", output_to_operand_aliasing={{0}: (2, {}), {1}: (3, {})} | custom-call | tf_op jit(solution)/shard_map/joingrad/pallas_call | solution.py:298
  119.0 6.0 %scattergrad.1 = bf16[3072,256]{1,0:T(8,128)(2,1)} custom-call(s32[24,2]{1,0:T(8,128)} %copy.15.nb_ref, s32[24]{0:T(128)} %cnt_ref.3, f32[3072,256]{1,0:T(8,128)} %get-tuple-element.13.right_ref, bf16[3072,256]{1,0:T(8,128)(2,1)} %get-tuple-element.14.ga, bf16[24,2,128,128]{3,2,1,0:T(8,128)(2,1)} %adj.1), custom_call_target="tpu_custom_call" | custom-call | tf_op jit(solution)/shard_map/scattergrad/pallas_call | solution.py:344
  125.0 0.6 fusion.4
  125.6 0.6 fusion.3
  (57 shorter events, 0.2 us)
Async XLA Ops:
  1.6 5.4 %collective-permute-start.1 = (bf16[2,128,256]{2,1,0:T(8,128)(2,1)S(1)}, bf16[2,128,256]{2,1,0:T(8,128)(2,1)S(1)}, u32[]{:S(2)}, u32[]{:S(2)}) collective-permute-start(bf16[2,128,256]{2,1,0:T(8,128)(2,1)S(1)} %bitcast.4), channel_id=1, source_target_pairs={{0,48},{1,49},{2,50},{3,51},{4,52},{5,53},{6,54},{7,55},{8,56},{9,... | collective-permute-start | bytes 393224 | tf_op jit(solution)/shard_map/ppermute | solution.py:25
  3.9 9.1 %collective-permute-start.2 = (bf16[2,128,256]{2,1,0:T(8,128)(2,1)S(1)}, bf16[2,128,256]{2,1,0:T(8,128)(2,1)S(1)}, u32[]{:S(2)}, u32[]{:S(2)}) collective-permute-start(bf16[2,128,256]{2,1,0:T(8,128)(2,1)S(1)} %bitcast.5), channel_id=1, source_target_pairs={{0,16},{1,17},{2,18},{3,19},{4,20},{5,21},{6,22},{7,23},{8,24},{9,... | collective-permute-start | bytes 393224 | tf_op jit(solution)/shard_map/ppermute | solution.py:25
  3.9 9.1 %collective-permute-start.3 = (bf16[2,128,256]{2,1,0:T(8,128)(2,1)S(1)}, bf16[2,128,256]{2,1,0:T(8,128)(2,1)S(1)}, u32[]{:S(2)}, u32[]{:S(2)}) collective-permute-start(bf16[2,128,256]{2,1,0:T(8,128)(2,1)S(1)} %bitcast.6), channel_id=1, source_target_pairs={{0,32},{1,33},{2,34},{3,35},{4,36},{5,37},{6,38},{7,39},{8,40},{9,... | collective-permute-start | bytes 393224 | tf_op jit(solution)/shard_map/ppermute | solution.py:25
  7.1 30.9 %copy-start = (bf16[4,128,256]{2,1,0:T(8,128)(2,1)}, bf16[4,128,256]{2,1,0:T(8,128)(2,1)S(1)}, u32[]{:S(2)}) copy-start(bf16[4,128,256]{2,1,0:T(8,128)(2,1)S(1)} %pad_maximum_fusion.refs_2_.refs_0_) | copy-start | bytes 786436
  7.1 12.5 %collective-permute-start.5 = (bf16[4,128,256]{2,1,0:T(8,128)(2,1)S(1)}, bf16[4,128,256]{2,1,0:T(8,128)(2,1)S(1)}, u32[]{:S(2)}, u32[]{:S(2)}) collective-permute-start(bf16[4,128,256]{2,1,0:T(8,128)(2,1)S(1)} %pad_maximum_fusion.refs_2_.refs_0_), channel_id=1, source_target_pairs={{0,14},{1,15},{2,0},{3,1},{4,2},{5,3},{6,4},{7,5},{8,6},{9,7},{10,... | collective-permute-start | bytes 786440 | tf_op jit(solution)/shard_map/ppermute | solution.py:25
  13.0 10.3 %collective-permute-start.4 = (bf16[4,128,256]{2,1,0:T(8,128)(2,1)S(1)}, bf16[4,128,256]{2,1,0:T(8,128)(2,1)S(1)}, u32[]{:S(2)}, u32[]{:S(2)}) collective-permute-start(bf16[4,128,256]{2,1,0:T(8,128)(2,1)S(1)} %pad_maximum_fusion.refs_2_.refs_0_), channel_id=1, source_target_pairs={{0,2},{1,3},{2,4},{3,5},{4,6},{5,7},{6,8},{7,9},{8,10},{9,11},{10,... | collective-permute-start | bytes 786440 | tf_op jit(solution)/shard_map/ppermute | solution.py:25
  13.1 24.9 %copy-start.1 = (bf16[4,128,256]{2,1,0:T(8,128)(2,1)}, bf16[4,128,256]{2,1,0:T(8,128)(2,1)S(1)}, u32[]{:S(2)}) copy-start(bf16[4,128,256]{2,1,0:T(8,128)(2,1)S(1)} %constant_dynamic-update-slice_fusion.refs_3_.refs_1_) | copy-start | bytes 786436
  13.1 12.1 %collective-permute-start.7 = (bf16[4,128,256]{2,1,0:T(8,128)(2,1)S(1)}, bf16[4,128,256]{2,1,0:T(8,128)(2,1)S(1)}, u32[]{:S(2)}, u32[]{:S(2)}) collective-permute-start(bf16[4,128,256]{2,1,0:T(8,128)(2,1)S(1)} %constant_dynamic-update-slice_fusion.refs_3_.refs_1_), channel_id=1, source_target_pairs={{0,14},{1,15},{2,0},{3,1},{4,2},{5,3},{6,4},{7,5},{8,6},{9,7},{10,... | collective-permute-start | bytes 786440 | tf_op jit(solution)/shard_map/ppermute | solution.py:25
  16.6 12.3 %collective-permute-start.6 = (bf16[4,128,256]{2,1,0:T(8,128)(2,1)S(1)}, bf16[4,128,256]{2,1,0:T(8,128)(2,1)S(1)}, u32[]{:S(2)}, u32[]{:S(2)}) collective-permute-start(bf16[4,128,256]{2,1,0:T(8,128)(2,1)S(1)} %constant_dynamic-update-slice_fusion.refs_3_.refs_1_), channel_id=1, source_target_pairs={{0,2},{1,3},{2,4},{3,5},{4,6},{5,7},{6,8},{7,9},{8,10},{9,11},{10,... | collective-permute-start | bytes 786440 | tf_op jit(solution)/shard_map/ppermute | solution.py:25
  19.6 18.4 %copy-start.3 = (bf16[4,128,256]{2,1,0:T(8,128)(2,1)}, bf16[4,128,256]{2,1,0:T(8,128)(2,1)S(1)}, u32[]{:S(2)}) copy-start(bf16[4,128,256]{2,1,0:T(8,128)(2,1)S(1)} %collective-permute-done.5.refs_5_.refs_3_) | copy-start | bytes 786436
  19.6 11.2 %collective-permute-start.9 = (bf16[4,128,256]{2,1,0:T(8,128)(2,1)S(1)}, bf16[4,128,256]{2,1,0:T(8,128)(2,1)S(1)}, u32[]{:S(2)}, u32[]{:S(2)}) collective-permute-start(bf16[4,128,256]{2,1,0:T(8,128)(2,1)S(1)} %collective-permute-done.5.refs_5_.refs_3_), channel_id=1, source_target_pairs={{0,14},{1,15},{2,0},{3,1},{4,2},{5,3},{6,4},{7,5},{8,6},{9,7},{10,... | collective-permute-start | bytes 786440 | tf_op jit(solution)/shard_map/ppermute | solution.py:25
  23.3 14.7 %copy-start.4 = (bf16[4,128,256]{2,1,0:T(8,128)(2,1)}, bf16[4,128,256]{2,1,0:T(8,128)(2,1)S(1)}, u32[]{:S(2)}) copy-start(bf16[4,128,256]{2,1,0:T(8,128)(2,1)S(1)} %collective-permute-done.4.refs_4_.refs_2_) | copy-start | bytes 786436
  23.3 10.9 %collective-permute-start.8 = (bf16[4,128,256]{2,1,0:T(8,128)(2,1)S(1)}, bf16[4,128,256]{2,1,0:T(8,128)(2,1)S(1)}, u32[]{:S(2)}, u32[]{:S(2)}) collective-permute-start(bf16[4,128,256]{2,1,0:T(8,128)(2,1)S(1)} %collective-permute-done.4.refs_4_.refs_2_), channel_id=1, source_target_pairs={{0,2},{1,3},{2,4},{3,5},{4,6},{5,7},{6,8},{7,9},{8,10},{9,11},{10,... | collective-permute-start | bytes 786440 | tf_op jit(solution)/shard_map/ppermute | solution.py:25
  25.2 12.8 %copy-start.5 = (bf16[4,128,256]{2,1,0:T(8,128)(2,1)}, bf16[4,128,256]{2,1,0:T(8,128)(2,1)S(1)}, u32[]{:S(2)}) copy-start(bf16[4,128,256]{2,1,0:T(8,128)(2,1)S(1)} %collective-permute-done.7.refs_7_.refs_5_) | copy-start | bytes 786436
  25.2 9.4 %collective-permute-start.11 = (bf16[4,128,256]{2,1,0:T(8,128)(2,1)S(1)}, bf16[4,128,256]{2,1,0:T(8,128)(2,1)S(1)}, u32[]{:S(2)}, u32[]{:S(2)}) collective-permute-start(bf16[4,128,256]{2,1,0:T(8,128)(2,1)S(1)} %collective-permute-done.7.refs_7_.refs_5_), channel_id=1, source_target_pairs={{0,14},{1,15},{2,0},{3,1},{4,2},{5,3},{6,4},{7,5},{8,6},{9,7},{10,... | collective-permute-start | bytes 786440 | tf_op jit(solution)/shard_map/ppermute | solution.py:25
  28.9 9.2 %copy-start.6 = (bf16[4,128,256]{2,1,0:T(8,128)(2,1)}, bf16[4,128,256]{2,1,0:T(8,128)(2,1)S(1)}, u32[]{:S(2)}) copy-start(bf16[4,128,256]{2,1,0:T(8,128)(2,1)S(1)} %collective-permute-done.6.refs_6_.refs_4_) | copy-start | bytes 786436
  28.9 9.1 %collective-permute-start.10 = (bf16[4,128,256]{2,1,0:T(8,128)(2,1)S(1)}, bf16[4,128,256]{2,1,0:T(8,128)(2,1)S(1)}, u32[]{:S(2)}, u32[]{:S(2)}) collective-permute-start(bf16[4,128,256]{2,1,0:T(8,128)(2,1)S(1)} %collective-permute-done.6.refs_6_.refs_4_), channel_id=1, source_target_pairs={{0,2},{1,3},{2,4},{3,5},{4,6},{5,7},{6,8},{7,9},{8,10},{9,11},{10,... | collective-permute-start | bytes 786440 | tf_op jit(solution)/shard_map/ppermute | solution.py:25
  28.9 1.4 %collective-permute-start = (s32[1,64]{1,0:T(1,128)}, s32[1,64]{1,0:T(1,128)S(1)}, u32[]{:S(2)}, u32[]{:S(2)}) collective-permute-start(s32[1,64]{1,0:T(1,128)} %want_ref.1), channel_id=1, source_target_pairs={{0,1},{1,0},{2,3},{3,2},{4,5},{5,4},{6,7},{7,6},{8,9},{9,8},{10,11... | collective-permute-start | bytes 776 | tf_op jit(solution)/shard_map/ppermute | solution.py:25
  30.3 7.8 %copy-start.20 = (s32[1,64]{1,0:T(1,128)}, s32[1,64]{1,0:T(1,128)S(1)}, u32[]{:S(2)}) copy-start(s32[1,64]{1,0:T(1,128)S(1)} %collective-permute-done.refs_0_) | copy-start | bytes 772
  30.8 7.2 %copy-start.7 = (bf16[4,128,256]{2,1,0:T(8,128)(2,1)}, bf16[4,128,256]{2,1,0:T(8,128)(2,1)S(1)}, u32[]{:S(2)}) copy-start(bf16[4,128,256]{2,1,0:T(8,128)(2,1)S(1)} %collective-permute-done.9.refs_9_.refs_7_) | copy-start | bytes 786436
  34.2 3.8 %copy-start.8 = (bf16[4,128,256]{2,1,0:T(8,128)(2,1)}, bf16[4,128,256]{2,1,0:T(8,128)(2,1)S(1)}, u32[]{:S(2)}) copy-start(bf16[4,128,256]{2,1,0:T(8,128)(2,1)S(1)} %collective-permute-done.8.refs_8_.refs_6_) | copy-start | bytes 786436
  34.6 3.5 %copy-start.9 = (bf16[4,128,256]{2,1,0:T(8,128)(2,1)}, bf16[4,128,256]{2,1,0:T(8,128)(2,1)S(1)}, u32[]{:S(2)}) copy-start(bf16[4,128,256]{2,1,0:T(8,128)(2,1)S(1)} %collective-permute-done.11.refs_11_.refs_9_) | copy-start | bytes 786436
  38.1 0.8 copy-start.10
  41.8 22.0 %copy-start.21 = (s32[24,2]{0,1:T(2,128)S(1)}, s32[24,2]{0,1:T(2,128)}, u32[]{:S(2)}) copy-start(s32[24,2]{0,1:T(2,128)} %param.12) | copy-start | bytes 580
  41.9 23.4 %collective-permute-start.12 = (bf16[20,128,256]{2,1,0:T(8,128)(2,1)}, bf16[20,128,256]{2,1,0:T(8,128)(2,1)S(1)}, u32[]{:S(2)}, u32[]{:S(2)}) collective-permute-start(bf16[20,128,256]{2,1,0:T(8,128)(2,1)} %pick.2), channel_id=1, source_target_pairs={{0,1},{1,0},{2,3},{3,2},{4,5},{5,4},{6,7},{7,6},{8,9},{9,8},{10,11... | collective-permute-start | bytes 3932168 | tf_op jit(solution)/shard_map/ppermute | solution.py:25
  42.0 10.7 %collective-permute-start.13 = (bf16[4,128,256]{2,1,0:T(8,128)(2,1)}, bf16[4,128,256]{2,1,0:T(8,128)(2,1)S(1)}, u32[]{:S(2)}, u32[]{:S(2)}) collective-permute-start(bf16[4,128,256]{2,1,0:T(8,128)(2,1)} %copy-done.8), channel_id=1, source_target_pairs={{0,2},{1,3},{2,4},{3,5},{4,6},{5,7},{6,8},{7,9},{8,10},{9,11},{10,... | collective-permute-start | bytes 786440 | tf_op jit(solution)/shard_map/ppermute | solution.py:25
  42.0 10.6 %collective-permute-start.16 = (bf16[4,128,256]{2,1,0:T(8,128)(2,1)}, bf16[4,128,256]{2,1,0:T(8,128)(2,1)S(1)}, u32[]{:S(2)}, u32[]{:S(2)}) collective-permute-start(bf16[4,128,256]{2,1,0:T(8,128)(2,1)} %copy-done.9), channel_id=1, source_target_pairs={{0,14},{1,15},{2,0},{3,1},{4,2},{5,3},{6,4},{7,5},{8,6},{9,7},{10,... | collective-permute-start | bytes 786440 | tf_op jit(solution)/shard_map/ppermute | solution.py:25
  45.3 12.6 %collective-permute-start.14 = (bf16[4,128,256]{2,1,0:T(8,128)(2,1)}, bf16[4,128,256]{2,1,0:T(8,128)(2,1)S(1)}, u32[]{:S(2)}, u32[]{:S(2)}) collective-permute-start(bf16[4,128,256]{2,1,0:T(8,128)(2,1)} %copy-done.7), channel_id=1, source_target_pairs={{0,14},{1,15},{2,0},{3,1},{4,2},{5,3},{6,4},{7,5},{8,6},{9,7},{10,... | collective-permute-start | bytes 786440 | tf_op jit(solution)/shard_map/ppermute | solution.py:25
  45.3 13.0 %collective-permute-start.15 = (bf16[4,128,256]{2,1,0:T(8,128)(2,1)}, bf16[4,128,256]{2,1,0:T(8,128)(2,1)S(1)}, u32[]{:S(2)}, u32[]{:S(2)}) collective-permute-start(bf16[4,128,256]{2,1,0:T(8,128)(2,1)} %copy-done.10), channel_id=1, source_target_pairs={{0,2},{1,3},{2,4},{3,5},{4,6},{5,7},{6,8},{7,9},{8,10},{9,11},{10,... | collective-permute-start | bytes 786440 | tf_op jit(solution)/shard_map/ppermute | solution.py:25
  52.6 5.6 %copy-start.11 = (bf16[4,128,256]{2,1,0:T(8,128)(2,1)}, bf16[4,128,256]{2,1,0:T(8,128)(2,1)S(1)}, u32[]{:S(2)}) copy-start(bf16[4,128,256]{2,1,0:T(8,128)(2,1)S(1)} %collective-permute-done.13.refs_2_.refs_10_) | copy-start | bytes 786436
  52.6 10.7 %collective-permute-start.18 = (bf16[4,128,256]{2,1,0:T(8,128)(2,1)S(1)}, bf16[4,128,256]{2,1,0:T(8,128)(2,1)S(1)}, u32[]{:S(2)}, u32[]{:S(2)}) collective-permute-start(bf16[4,128,256]{2,1,0:T(8,128)(2,1)S(1)} %collective-permute-done.13.refs_2_.refs_10_), channel_id=1, source_target_pairs={{0,2},{1,3},{2,4},{3,5},{4,6},{5,7},{6,8},{7,9},{8,10},{9,11},{10,... | collective-permute-start | bytes 786440 | tf_op jit(solution)/shard_map/ppermute | solution.py:25
  52.6 5.6 %copy-start.12 = (bf16[4,128,256]{2,1,0:T(8,128)(2,1)}, bf16[4,128,256]{2,1,0:T(8,128)(2,1)S(1)}, u32[]{:S(2)}) copy-start(bf16[4,128,256]{2,1,0:T(8,128)(2,1)S(1)} %collective-permute-done.16.refs_5_.refs_13_) | copy-start | bytes 786436
  52.7 10.7 %collective-permute-start.20 = (bf16[4,128,256]{2,1,0:T(8,128)(2,1)S(1)}, bf16[4,128,256]{2,1,0:T(8,128)(2,1)S(1)}, u32[]{:S(2)}, u32[]{:S(2)}) collective-permute-start(bf16[4,128,256]{2,1,0:T(8,128)(2,1)S(1)} %collective-permute-done.16.refs_5_.refs_13_), channel_id=1, source_target_pairs={{0,14},{1,15},{2,0},{3,1},{4,2},{5,3},{6,4},{7,5},{8,6},{9,7},{10,... | collective-permute-start | bytes 786440 | tf_op jit(solution)/shard_map/ppermute | solution.py:25
  57.9 0.7 copy-start.13
  58.6 0.7 copy-start.14
  61.9 3.4 %collective-permute-start.17 = (bf16[8,128,256]{2,1,0:T(8,128)(2,1)}, bf16[8,128,256]{2,1,0:T(8,128)(2,1)S(1)}, u32[]{:S(2)}, u32[]{:S(2)}) collective-permute-start(bf16[8,128,256]{2,1,0:T(8,128)(2,1)} %pick.3), channel_id=1, source_target_pairs={{0,1},{1,0},{2,3},{3,2},{4,5},{5,4},{6,7},{7,6},{8,9},{9,8},{10,11... | collective-permute-start | bytes 1572872 | tf_op jit(solution)/shard_map/ppermute | solution.py:25
  63.3 1.9 %copy-start.16 = (bf16[4,128,256]{2,1,0:T(8,128)(2,1)}, bf16[4,128,256]{2,1,0:T(8,128)(2,1)S(1)}, u32[]{:S(2)}) copy-start(bf16[4,128,256]{2,1,0:T(8,128)(2,1)S(1)} %collective-permute-done.18.refs_14_) | copy-start | bytes 786436
  63.3 1.5 %collective-permute-start.19 = (bf16[4,128,256]{2,1,0:T(8,128)(2,1)S(1)}, bf16[4,128,256]{2,1,0:T(8,128)(2,1)S(1)}, u32[]{:S(2)}, u32[]{:S(2)}) collective-permute-start(bf16[4,128,256]{2,1,0:T(8,128)(2,1)S(1)} %collective-permute-done.18.refs_14_), channel_id=1, source_target_pairs={{0,1},{1,0},{2,3},{3,2},{4,5},{5,4},{6,7},{7,6},{8,9},{9,8},{10,11... | collective-permute-start | bytes 786440 | tf_op jit(solution)/shard_map/ppermute | solution.py:25
  63.3 1.9 %copy-start.17 = (bf16[4,128,256]{2,1,0:T(8,128)(2,1)}, bf16[4,128,256]{2,1,0:T(8,128)(2,1)S(1)}, u32[]{:S(2)}) copy-start(bf16[4,128,256]{2,1,0:T(8,128)(2,1)S(1)} %collective-permute-done.20.refs_15_) | copy-start | bytes 786436
  63.3 1.9 %collective-permute-start.21 = (bf16[4,128,256]{2,1,0:T(8,128)(2,1)S(1)}, bf16[4,128,256]{2,1,0:T(8,128)(2,1)S(1)}, u32[]{:S(2)}, u32[]{:S(2)}) collective-permute-start(bf16[4,128,256]{2,1,0:T(8,128)(2,1)S(1)} %collective-permute-done.20.refs_15_), channel_id=1, source_target_pairs={{0,1},{1,0},{2,3},{3,2},{4,5},{5,4},{6,7},{7,6},{8,9},{9,8},{10,11... | collective-permute-start | bytes 786440 | tf_op jit(solution)/shard_map/ppermute | solution.py:25
  64.9 0.7 copy-start.18
  65.2 0.7 copy-start.19
  65.2 0.9 copy-start.15
  66.1 1.1 copy-start.2
  80.0 2.6 %collective-permute-start.22 = (f32[32,8,768]{2,1,0:T(8,128)}, f32[32,8,768]{2,1,0:T(8,128)S(1)}, u32[]{:S(2)}, u32[]{:S(2)}) collective-permute-start(f32[32,8,768]{2,1,0:T(8,128)} %get-tuple-element.16), channel_id=1, source_target_pairs={{0,1},{1,0},{2,3},{3,2},{4,5},{5,4},{6,7},{7,6},{8,9},{9,8},{10,11... | collective-permute-start | bytes 2359304 | tf_op jit(solution)/shard_map/ppermute | solution.py:25
  83.8 5.8 %collective-permute-start.23 = (bf16[8,8,768]{2,1,0:T(8,128)(2,1)S(1)}, bf16[8,8,768]{2,1,0:T(8,128)(2,1)S(1)}, u32[]{:S(2)}, u32[]{:S(2)}) collective-permute-start(bf16[8,8,768]{2,1,0:T(8,128)(2,1)S(1)} %get-tuple-element.19), channel_id=1, source_target_pairs={{0,16},{1,17},{2,18},{3,19},{4,20},{5,21},{6,22},{7,23},{8,24},{9,... | collective-permute-start | bytes 294920 | tf_op jit(solution)/shard_map/ppermute | solution.py:25
  85.3 7.2 %collective-permute-start.25 = (bf16[8,8,768]{2,1,0:T(8,128)(2,1)S(1)}, bf16[8,8,768]{2,1,0:T(8,128)(2,1)S(1)}, u32[]{:S(2)}, u32[]{:S(2)}) collective-permute-start(bf16[8,8,768]{2,1,0:T(8,128)(2,1)S(1)} %get-tuple-element.20), channel_id=1, source_target_pairs={{0,32},{1,33},{2,34},{3,35},{4,36},{5,37},{6,38},{7,39},{8,40},{9,... | collective-permute-start | bytes 294920 | tf_op jit(solution)/shard_map/ppermute | solution.py:25
  87.5 6.2 %collective-permute-start.24 = (bf16[8,8,768]{2,1,0:T(8,128)(2,1)S(1)}, bf16[8,8,768]{2,1,0:T(8,128)(2,1)S(1)}, u32[]{:S(2)}, u32[]{:S(2)}) collective-permute-start(bf16[8,8,768]{2,1,0:T(8,128)(2,1)S(1)} %get-tuple-element.21), channel_id=1, source_target_pairs={{0,48},{1,49},{2,50},{3,51},{4,52},{5,53},{6,54},{7,55},{8,56},{9,... | collective-permute-start | bytes 294920 | tf_op jit(solution)/shard_map/ppermute | solution.py:25
  106.7 18.3 %collective-permute-start.28 = (f32[8,768]{1,0:T(8,128)S(1)}, f32[8,768]{1,0:T(8,128)S(1)}, u32[]{:S(2)}, u32[]{:S(2)}) collective-permute-start(f32[8,768]{1,0:T(8,128)S(1)} %convert_reduce_fusion), channel_id=1, source_target_pairs={{0,192},{64,128},{128,64},{192,0},{1,193},{65,129},{129,65},{193,1... | collective-permute-start | bytes 73736 | tf_op jit(solution)/shard_map/ppermute | solution.py:377
  109.7 15.2 %collective-permute-start.27 = (f32[8,768]{1,0:T(8,128)S(1)}, f32[8,768]{1,0:T(8,128)S(1)}, u32[]{:S(2)}, u32[]{:S(2)}) collective-permute-start(f32[8,768]{1,0:T(8,128)S(1)} %convert_reduce_fusion), channel_id=1, source_target_pairs={{0,128},{64,192},{128,0},{192,64},{1,129},{65,193},{129,1},{193,65... | collective-permute-start | bytes 73736 | tf_op jit(solution)/shard_map/ppermute | solution.py:377
  110.5 14.5 %collective-permute-start.26 = (f32[8,768]{1,0:T(8,128)S(1)}, f32[8,768]{1,0:T(8,128)S(1)}, u32[]{:S(2)}, u32[]{:S(2)}) collective-permute-start(f32[8,768]{1,0:T(8,128)S(1)} %convert_reduce_fusion), channel_id=1, source_target_pairs={{0,64},{64,0},{128,192},{192,128},{1,65},{65,1},{129,193},{193,129... | collective-permute-start | bytes 73736 | tf_op jit(solution)/shard_map/ppermute | solution.py:377
